TPU v7x, 32 devices: a whole 2x2x4 slice. The times are simulated.
32 devices in a mesh: groups: 2 (over x), pos: 8 (over z, y), mp: 2 (over core).
Axes of the slice: x: 2, y: 2, z: 4, core: 2. Of those that a mesh axis runs over, the one named last changes fastest.
Arguments:
- gate_stream: bfloat16 [8192, 4096], P(('groups', 'pos'), 'mp'), parts along dimension 0, may hold values from -6 to 6
- key_stream: bfloat16 [8192, 4096], P(('groups', 'pos'), 'mp'), parts along dimension 0, may hold values from -6 to 6
- value_stream: bfloat16 [8192, 4096], P(('groups', 'pos'), 'mp'), parts along dimension 0, may hold values from -6 to 6
- filters: float32 [4096, 128], P('mp')
- temps: float32 [32], P('mp'), may hold values from 4 to 24
- queries: bfloat16 [32, 256, 4096], P('groups', 'pos', 'mp'), parts along dimension 0, may hold values from -6 to 6
- blocks: int32 [32], P('groups'), parts along dimension 0, may hold values from 0 to 7, as said below
- sites: int32 [32], P('groups'), parts along dimension 0, may hold values from 128 to 4095, as said below
Outputs:
- hyena_out: bfloat16 [8192, 4096], P(('groups', 'pos'), 'mp'), parts along dimension 0
- attended: bfloat16 [32, 256, 4096], P('groups', 'pos', 'mp'), parts along dimension 0
There are 2 independent parts, one for each index of `groups`. A program takes and returns all parts, laid end to end along the dimension named above; an argument that names none is the same for every part. Nothing has to cross between parts.
Inputs may be any that keep to these rules, and one draw needn't show every extreme that they name: `blocks`: A block is the 512 reference positions of one index of pos. Exactly one block is named by exactly 4 windows; every other block by at most two windows, and some block by exactly two. sites[w] - 512 * blocks[w] lies from 128 to 511.
All inputs are finite; a program needn't handle non-finite values.
Results may differ from a plain program's by a relative error of at most 0.01.
Values may be sent and summed in bfloat16 or wider, within the bound.
A program may use at most 128 MiB of HBM per device.

v0:
```python
import jax
import jax.numpy as jnp
from jax import lax
from jax.sharding import PartitionSpec as P

HEAD_DIM = 128
HOT = 4


def shifted(value, axis, by):
    peers = lax.axis_size(axis)
    pairs = [(i, i + by) for i in range(peers) if 0 <= i + by < peers]
    return lax.ppermute(value, axis, pairs)


def causal_mix(extended, filters):
    kernel = jnp.flip(filters.T, 0)[:, None, :]
    mixed = lax.conv_general_dilated(
        extended.astype(jnp.float32)[None],
        kernel,
        (1,),
        "VALID",
        dimension_numbers=("NWC", "WIO", "NWC"),
        feature_group_count=filters.shape[0],
        precision=lax.Precision.HIGHEST,
    )
    return mixed[0]


def head_norm(block, heads):
    shaped = block.astype(jnp.float32).reshape(block.shape[:-1] + (heads, HEAD_DIM))
    scale = lax.rsqrt(jnp.mean(shaped * shaped, axis=-1, keepdims=True) + 1e-06)
    return (shaped * scale).reshape(block.shape).astype(jnp.bfloat16)


def attend_slot(query_rows, key_rows, value_rows, offset, temps):
    heads = temps.shape[0]
    length = query_rows.shape[0]
    positions = key_rows.shape[0]
    qnorm = head_norm(query_rows, heads).reshape(length, heads, HEAD_DIM)
    keyed = key_rows.reshape(positions, heads, HEAD_DIM)
    valued = value_rows.reshape(positions, heads, HEAD_DIM)
    scores = (
        jnp.einsum("qhd,khd->hqk", qnorm, keyed, preferred_element_type=jnp.float32)
        * (temps / HEAD_DIM)[:, None, None]
    )
    live = lax.broadcasted_iota(jnp.int32, (1, 1, positions), 2) < offset
    weights = jnp.where(live, jnp.exp(scores), 0.0)
    total = jnp.sum(weights, axis=-1)
    numer = jnp.einsum(
        "hqk,khd->qhd", weights.astype(jnp.bfloat16), valued, preferred_element_type=jnp.float32
    )
    return (numer / total.T[:, :, None]).reshape(length, heads * HEAD_DIM).astype(jnp.bfloat16)


def shards(gate_stream, key_stream, value_stream, filters, temps, queries, blocks, sites):
    rows, chans = gate_stream.shape
    taps = filters.shape[1]
    product = (key_stream.astype(jnp.float32) * value_stream.astype(jnp.float32)).astype(
        jnp.bfloat16
    )
    earlier = shifted(product[rows - taps :], "pos", 1)
    extended = jnp.concatenate([earlier[1:], product], 0)
    mixed = causal_mix(extended, filters)
    hyena_out = (gate_stream.astype(jnp.float32) * mixed).astype(jnp.bfloat16)
    keys = head_norm(hyena_out, temps.shape[0])
    count = lax.axis_size("pos")
    me = lax.axis_index("pos")
    windows = blocks.shape[0]
    order = jnp.arange(windows)
    before = order[None, :] < order[:, None]
    same = (blocks[:, None] == blocks[None, :]) & before
    within = jnp.sum(same, axis=1)
    slot_count = HOT
    slot_ids = jnp.arange(slot_count)
    tok_rows = queries.shape[1]
    select = (blocks[None, None, :] == jnp.arange(count)[None, :, None]) & (
        within[None, None, :] == slot_ids[:, None, None]
    )
    outgoing = jnp.dot(
        select.reshape(slot_count * count, windows).astype(jnp.bfloat16),
        queries.reshape(windows, tok_rows * chans),
        preferred_element_type=jnp.float32,
    )
    outgoing = outgoing.astype(jnp.bfloat16).reshape(slot_count, count * tok_rows, chans)
    arrived = lax.all_to_all(outgoing, "pos", split_axis=1, concat_axis=1, tiled=True)
    mine = (blocks == me)[None, :] & (within[None, :] == slot_ids[:, None])
    offsets = jnp.sum(jnp.where(mine, sites[None, :] - blocks[None, :] * rows, 0), axis=1)
    offsets = jnp.where(jnp.any(mine, axis=1), offsets, rows)

    def one_slot(item):
        return attend_slot(item[0], keys, hyena_out, item[1], temps)

    results = lax.map(one_slot, (arrived, offsets))
    returned = lax.all_to_all(results, "pos", split_axis=1, concat_axis=0, tiled=True)
    pick = blocks[:, None] * slot_count + within[:, None] == jnp.arange(count * slot_count)[None, :]
    attended = jnp.dot(
        pick.astype(jnp.bfloat16),
        returned.reshape(count * slot_count, tok_rows * chans),
        preferred_element_type=jnp.float32,
    )
    attended = attended.astype(jnp.bfloat16).reshape(windows, tok_rows, chans)
    return (hyena_out, attended)


def solution(mesh):
    placed = (
        P(("groups", "pos"), "mp"),
        P(("groups", "pos"), "mp"),
        P(("groups", "pos"), "mp"),
        P("mp", None),
        P("mp"),
        P("groups", "pos", "mp"),
        P("groups"),
        P("groups"),
    )
    return jax.shard_map(
        shards,
        mesh=mesh,
        in_specs=placed,
        out_specs=(P(("groups", "pos"), "mp"), P("groups", "pos", "mp")),
        check_vma=False,
    )
```

profile of v0, /device:TPU:6, one launch (start us, length us, event | category | flops | bytes accessed | tf_op | source)
XLA Modules:
  0.0 290.6 jit_solution(6040972376619216045)
XLA Ops:
  0.6 3.0 %multiply_convert_fusion.1 = bf16[512,2048]{1,0:T(8,128)(2,1)S(1)} fusion(bf16[512,2048]{1,0:T(8,128)(2,1)} %param.12, bf16[512,2048]{1,0:T(8,128)(2,1)} %param.11), kind=kLoop, calls=%fused_computation.31 | loop fusion | flops 4194304 | bytes 6291456 | tf_op jit(solution)/shard_map/convert_element_type | solution.py:59
  3.7 0.8 slice.8
  4.5 3.4 %collective-permute-start = (bf16[128,2048]{1,0:T(8,128)(2,1)}, bf16[128,2048]{1,0:T(8,128)(2,1)}, u32[]{:S(2)}, u32[]{:S(2)}) collective-permute-start(bf16[128,2048]{1,0:T(8,128)(2,1)} %slice.8), channel_id=1, source_target_pairs={{0,2},{2,4},{4,6},{6,8},{8,10},{10,12},{12,14},{1,3},{3,5},{5,7},{... | collective-permute-start | bytes 1572872 | tf_op jit(solution)/shard_map/ppermute | solution.py:13
  8.1 2.7 copy.71
  11.0 3.2 %convolution_convert_fusion = bf16[32,65536]{1,0:T(8,128)(2,1)} fusion(bf16[16,65536]{1,0:T(8,128)(2,1)S(1)} %bitcast.84, pred[4,16]{1,0:T(4,128)(4,1)S(1)} %get-tuple-element.102, pred[8,16]{1,0:T(8,128)(4,1)S(1)} %iota_compare_fusion.4), kind=kOutput, calls=%fused_computation.21 | convolution fusion | flops 69206528 | bytes 6291648 | tf_op jit(solution)/shard_map/dot_general | solution.py:80
  14.2 5.6 %reshape.143 = bf16[4,256,2048]{2,1,0:T(8,128)(2,1)} reshape(bf16[32,65536]{1,0:T(8,128)(2,1)} %convolution_convert_fusion) | data formatting | bytes 8388608 | tf_op jit(solution)/shard_map/reshape | solution.py:85
  19.8 7.3 %copy.60 = bf16[4,256,2048]{2,0,1:T(4,128)(2,1)} copy(bf16[4,256,2048]{2,1,0:T(8,128)(2,1)} %reshape.143) | data formatting | bytes 8388608 | tf_op jit(solution)/shard_map/reshape | solution.py:85
  27.1 5.8 %all-to-all-start = ((bf16[4,256,2048]{2,0,1:T(4,128)(2,1)}), bf16[4,256,2048]{2,0,1:T(4,128)(2,1)}, u32[]{:S(2)}, u32[]{:S(2)}) async-start(bf16[4,256,2048]{2,0,1:T(4,128)(2,1)} %copy.60), calls=%async_computation | async-start | bytes 8388608 | tf_op jit(solution)/shard_map/all_to_all | solution.py:86
  32.9 7.5 %rev.4 = f32[128,2048]{0,1:T(8,128)S(1)} reverse(f32[128,2048]{0,1:T(8,128)} %bitcast.89), dimensions={0} | reverse | bytes 2097152 | tf_op jit(solution)/shard_map/jit(_flip)/rev | solution.py:17
  40.4 1.9 copy.59
  42.3 0.5 multiply_add_fusion
  43.0 1.2 slice.9
  44.1 0.6 maximum_bitcast_fusion
  44.8 45.5 %fusion.15 = f32[1,512,2048]{2,0,1:T(1,128)S(1)} fusion(f32[128,1,2048]{2,1,0:T(1,128)S(1)} %copy-done.3, bf16[1,639,2048]{2,1,0:T(8,128)(2,1)S(1)} %maximum_bitcast_fusion), kind=kOutput, calls=%fused_computation.25 | convolution fusion | flops 1610612736 | bytes 7860224 | tf_op jit(solution)/shard_map/conv_general_dilated | solution.py:18
  90.3 2.3 fusion.17
  92.6 2.9 copy.72
  95.5 3.4 %reduce_sum.47 = f32[512,16]{1,0:T(8,128)S(1)} reduce(f32[512,16,128]{2,1,0:T(8,128)} %bitcast.79, f32[]{:T(128)} %constant.41.clone.1), dimensions={2}, to_apply=%region_3.4 | reduce | flops 1040384 | bytes 4227076 | tf_op jit(solution)/shard_map/reduce_sum | solution.py:32
  99.1 2.6 copy.64
  101.7 1.1 mul.62
  102.8 3.1 %fusion.18 = bf16[512,2048]{1,0:T(8,128)(2,1)} fusion(bf16[512,2048]{1,0:T(8,128)(2,1)S(1)} %get-tuple-element.97, f32[64,8,16,128]{3,2,1,0:T(8,128)S(1)} %bitcast.80), kind=kLoop, calls=%fused_computation.28 | loop fusion | flops 3145728 | bytes 8388608 | tf_op jit(solution)/shard_map/convert_element_type | solution.py:33
  105.9 19.8 %all-to-all-done = bf16[4,256,2048]{2,0,1:T(4,128)(2,1)} async-done(((bf16[4,256,2048]{2,0,1:T(4,128)(2,1)}), bf16[4,256,2048]{2,0,1:T(4,128)(2,1)}, u32[]{:S(2)}, u32[]{:S(2)}) %all-to-all-start) | async-done | bytes 4194336 | tf_op jit(solution)/shard_map/all_to_all | solution.py:86
  125.7 6.4 %copy.63 = bf16[4,256,2048]{2,1,0:T(8,128)(2,1)} copy(bf16[4,256,2048]{2,0,1:T(4,128)(2,1)} %all-to-all-done) | data formatting | bytes 8388608 | tf_op jit(solution)/shard_map/while | solution.py:94
  132.1 45.2 %while.10 = (s32[]{:T(128)}, bf16[4,256,2048]{1,2,0:T(8,128)(2,1)}, s32[4]{0:T(128)S(1)}, bf16[4,256,2048]{2,1,0:T(8,128)(2,1)}, bf16[512,2048]{1,0:T(8,128)(2,1...) while((s32[]{:T(128)}, bf16[4,256,2048]{1,2,0:T(8,128)(2,1)}, s32[4]{0:T(128)S(1)}, ...), condition=%wide.region_7.8_spmd, body=%wide.region_4.7_spmd.sunk | while | flops 1089995264 | bytes 46303620 | solution.py:94
  132.1 1.5 convert_bitcast_fusion.2
  133.6 0.4 copy.98
  133.9 0.6 multiply_reduce_fusion.2
  134.7 0.9 multiply_convert_fusion.3
  135.6 0.7 dynamic_slice.12
  136.3 0.6 iota_compare_fusion.7
  136.9 3.6 %fusion.40 = (f32[16,256]{1,0:T(8,128)S(1)}, f32[16,256,512]{2,1,0:T(8,128)S(1)}) fusion(f32[16]{0:T(128)S(1)} %broadcast_multiply_fusion.2, pred[512]{0:T(512)(128)(4,1)S(1)} %iota_compare_fusion.7, bf16[256,16,128]{2,1,0:T(8,128)(2,1)S(1)} %multiply_convert_fusion.3, bf16[512,2048]{1,0:T(8,128)(2,1)} %get-tuple-element.171), kind=kOutput, calls=%fused_computation.1.clone.1 | convolution fusion | flops 543158272 | bytes 11551296 | tf_op jit(solution)/shard_map/while/body/eval_jaxpr/qhd,khd->hqk/dot_general | solution.py:44
  140.6 1.7 fusion.41
  142.3 1.0 constant_dynamic-update-slice_fusion.2
  143.4 1.5 convert_bitcast_fusion.2
  144.8 0.4 copy.98
  145.2 0.6 multiply_reduce_fusion.2
  146.0 0.9 multiply_convert_fusion.3
  146.9 0.7 dynamic_slice.12
  147.6 0.6 iota_compare_fusion.7
  148.2 3.6 %fusion.40 = (f32[16,256]{1,0:T(8,128)S(1)}, f32[16,256,512]{2,1,0:T(8,128)S(1)}) fusion(f32[16]{0:T(128)S(1)} %broadcast_multiply_fusion.2, pred[512]{0:T(512)(128)(4,1)S(1)} %iota_compare_fusion.7, bf16[256,16,128]{2,1,0:T(8,128)(2,1)S(1)} %multiply_convert_fusion.3, bf16[512,2048]{1,0:T(8,128)(2,1)} %get-tuple-element.171), kind=kOutput, calls=%fused_computation.1.clone.1 | convolution fusion | flops 543158272 | bytes 11551296 | tf_op jit(solution)/shard_map/while/body/eval_jaxpr/qhd,khd->hqk/dot_general | solution.py:44
  151.9 1.7 fusion.41
  153.6 1.1 constant_dynamic-update-slice_fusion.2
  154.7 1.5 convert_bitcast_fusion.2
  156.5 0.6 multiply_reduce_fusion.2
  157.4 0.9 multiply_convert_fusion.3
  158.2 0.7 dynamic_slice.12
  158.9 0.6 iota_compare_fusion.7
  159.5 3.6 %fusion.40 = (f32[16,256]{1,0:T(8,128)S(1)}, f32[16,256,512]{2,1,0:T(8,128)S(1)}) fusion(f32[16]{0:T(128)S(1)} %broadcast_multiply_fusion.2, pred[512]{0:T(512)(128)(4,1)S(1)} %iota_compare_fusion.7, bf16[256,16,128]{2,1,0:T(8,128)(2,1)S(1)} %multiply_convert_fusion.3, bf16[512,2048]{1,0:T(8,128)(2,1)} %get-tuple-element.171), kind=kOutput, calls=%fused_computation.1.clone.1 | convolution fusion | flops 543158272 | bytes 11551296 | tf_op jit(solution)/shard_map/while/body/eval_jaxpr/qhd,khd->hqk/dot_general | solution.py:44
  163.2 1.7 fusion.41
  164.9 1.1 constant_dynamic-update-slice_fusion.2
  166.0 1.5 convert_bitcast_fusion.2
  167.9 0.6 multiply_reduce_fusion.2
  168.7 0.9 multiply_convert_fusion.3
  169.5 0.7 dynamic_slice.12
  170.2 0.6 iota_compare_fusion.7
  170.8 3.6 %fusion.40 = (f32[16,256]{1,0:T(8,128)S(1)}, f32[16,256,512]{2,1,0:T(8,128)S(1)}) fusion(f32[16]{0:T(128)S(1)} %broadcast_multiply_fusion.2, pred[512]{0:T(512)(128)(4,1)S(1)} %iota_compare_fusion.7, bf16[256,16,128]{2,1,0:T(8,128)(2,1)S(1)} %multiply_convert_fusion.3, bf16[512,2048]{1,0:T(8,128)(2,1)} %get-tuple-element.171), kind=kOutput, calls=%fused_computation.1.clone.1 | convolution fusion | flops 543158272 | bytes 11551296 | tf_op jit(solution)/shard_map/while/body/eval_jaxpr/qhd,khd->hqk/dot_general | solution.py:44
  174.5 1.7 fusion.41
  176.2 1.0 constant_dynamic-update-slice_fusion.2
  177.3 8.0 %copy.65 = bf16[4,256,2048]{2,0,1:T(4,128)(2,1)} copy(bf16[4,256,2048]{1,2,0:T(8,128)(2,1)} %get-tuple-element.39) | data formatting | bytes 8388608 | tf_op jit(solution)/shard_map/while | solution.py:94
  185.2 96.9 %all_to_all.20 = bf16[4,256,2048]{2,0,1:T(4,128)(2,1)S(1)} all-to-all(bf16[4,256,2048]{2,0,1:T(4,128)(2,1)} %copy.65), channel_id=1, replica_groups=mesh['groups'=2,'pos'=8,'mp'=2] {'pos'}, dimensions={1} | all-to-all | bytes 8388608 | tf_op jit(solution)/shard_map/all_to_all | solution.py:95
  282.1 2.3 copy.66
  284.4 0.6 copy.67
  285.0 2.3 copy.74
  287.4 0.8 convolution_convert_fusion.1
  288.2 2.5 copy.75
  (51 shorter events, 2.2 us)
Async XLA Ops:
  0.6 7.3 %copy-start.5 = (s32[16]{0:T(128)S(1)}, s32[16]{0:T(128)}, u32[]{:S(2)}) copy-start(s32[16]{0:T(128)} %param.16) | copy-start | bytes 196
  4.5 38.5 %collective-permute-start = (bf16[128,2048]{1,0:T(8,128)(2,1)}, bf16[128,2048]{1,0:T(8,128)(2,1)}, u32[]{:S(2)}, u32[]{:S(2)}) collective-permute-start(bf16[128,2048]{1,0:T(8,128)(2,1)} %slice.8), channel_id=1, source_target_pairs={{0,2},{2,4},{4,6},{6,8},{8,10},{10,12},{12,14},{1,3},{3,5},{5,7},{... | collective-permute-start | bytes 1572872 | tf_op jit(solution)/shard_map/ppermute | solution.py:13
  27.1 98.5 %all-to-all-start = ((bf16[4,256,2048]{2,0,1:T(4,128)(2,1)}), bf16[4,256,2048]{2,0,1:T(4,128)(2,1)}, u32[]{:S(2)}, u32[]{:S(2)}) async-start(bf16[4,256,2048]{2,0,1:T(4,128)(2,1)} %copy.60), calls=%async_computation | async-start | bytes 8388608 | tf_op jit(solution)/shard_map/all_to_all | solution.py:86
  32.9 9.4 %copy-start.6 = (s32[16]{0:T(128)S(1)}, s32[16]{0:T(128)}, u32[]{:S(2)}) copy-start(s32[16]{0:T(128)} %param.17) | copy-start | bytes 196
  42.3 2.5 copy-start.3
  44.8 45.5 %copy-start.2 = (bf16[512,2048]{1,0:T(8,128)(2,1)S(1)}, bf16[512,2048]{1,0:T(8,128)(2,1)}, u32[]{:S(2)}) copy-start(bf16[512,2048]{1,0:T(8,128)(2,1)} %param.10) | copy-start | bytes 6291460
  92.6 10.2 %copy-start = (bf16[512,2048]{1,0:T(8,128)(2,1)}, bf16[512,2048]{1,0:T(8,128)(2,1)S(1)}, u32[]{:S(2)}) copy-start(bf16[512,2048]{1,0:T(8,128)(2,1)S(1)} %get-tuple-element.97) | copy-start | bytes 6291460
  105.9 26.2 %copy-start.7 = (f32[16]{0:T(128)S(1)}, f32[16]{0:T(128)}, u32[]{:S(2)}) copy-start(f32[16]{0:T(128)} %param.14) | copy-start | bytes 196
  136.9 3.7 %copy-start.1 = (bf16[512,2048]{0,1:T(8,128)(2,1)S(1)}, bf16[512,2048]{0,1:T(8,128)(2,1)}, u32[]{:S(2)}) copy-start(bf16[512,2048]{0,1:T(8,128)(2,1)} %get-tuple-element.173) | copy-start | bytes 6291460 | tf_op jit(solution)/shard_map/while
  148.2 3.6 %copy-start.1 = (bf16[512,2048]{0,1:T(8,128)(2,1)S(1)}, bf16[512,2048]{0,1:T(8,128)(2,1)}, u32[]{:S(2)}) copy-start(bf16[512,2048]{0,1:T(8,128)(2,1)} %get-tuple-element.173) | copy-start | bytes 6291460 | tf_op jit(solution)/shard_map/while
  159.5 3.6 %copy-start.1 = (bf16[512,2048]{0,1:T(8,128)(2,1)S(1)}, bf16[512,2048]{0,1:T(8,128)(2,1)}, u32[]{:S(2)}) copy-start(bf16[512,2048]{0,1:T(8,128)(2,1)} %get-tuple-element.173) | copy-start | bytes 6291460 | tf_op jit(solution)/shard_map/while
  170.8 3.6 %copy-start.1 = (bf16[512,2048]{0,1:T(8,128)(2,1)S(1)}, bf16[512,2048]{0,1:T(8,128)(2,1)}, u32[]{:S(2)}) copy-start(bf16[512,2048]{0,1:T(8,128)(2,1)} %get-tuple-element.173) | copy-start | bytes 6291460 | tf_op jit(solution)/shard_map/while
  285.0 2.4 copy-start.4
where the time goes:
time: 293 us; the launch traced here: 291 us
  blocking collectives  96.9 us (33%)
  matrix products  70.8 us (24%)
  local copies, waits for them, and re-layouts  65.1 us (22%)
  other arithmetic  27.7 us (9%)
  waiting for transfers between devices  19.8 us (7%)
  starting transfers between devices  9.21 us (3%)
    all_to_all x1, blocking collectives, shards(): lax.all_to_all(results, 'pos', split_axis=1, concat_axis=0, tiled=True)  96.9 us
    conv_general_dilated x1, matrix products, causal_mix(): lax.conv_general_dilated(extended.astype(jnp.float32)[None], kernel, (1,)...  45.5 us
    all_to_all x1, waiting for transfers between devices, shards(): lax.all_to_all(outgoing, 'pos', split_axis=1, concat_axis=1, tiled=True)  19.8 us
    while x3, local copies, waits for them, and re-layouts, shards(): results = lax.map(one_slot, (arrived, offsets))  16.9 us
    dot_general x4, matrix products, attend_slot(): jnp.einsum('qhd,khd->hqk', qnorm, keyed, preferred_element_type=jnp.float32)  14.5 us
    reshape x2, local copies, waits for them, and re-layouts, shards(): outgoing.astype(jnp.bfloat16).reshape(slot_count, count * tok_rows, chans)  13 us
    unnamed x18, local copies, waits for them, and re-layouts  10.5 us
    rev x1, local copies, waits for them, and re-layouts, causal_mix(): kernel = jnp.flip(filters.T, 0)[:, None, :]  7.51 us
  transfers between devices with their start and end apart: 2, of which 1 were waited for; matrix products, arithmetic and copies ran while one was open for 32% of the time, Pallas kernels for 0%

commit v1 on v0

v1 whole, which is shorter than its diff:
```python
import functools
import math

import jax
import jax.numpy as jnp
import numpy as np
from jax import lax
from jax.experimental import pallas as pl
from jax.experimental.pallas import tpu as pltpu
from jax.sharding import PartitionSpec as P

HEAD_DIM = 128
LOG2E = math.log2(math.e)


def transforms(taps):
    size = 2 * taps
    freq = (np.arange(taps) + 0.5) * (2 * np.pi / size)
    grid = freq[:, None] * np.arange(size)[None, :]
    both = np.concatenate([np.cos(grid), np.sin(grid)], 0)
    forward = both / size
    short = both[:, :taps] / taps
    inverse = both[:, taps:].T * taps * 2.0
    cast = lambda a: jnp.asarray(a, jnp.bfloat16)
    return cast(forward), cast(np.concatenate([short, short], 1)), cast(inverse)


def unit(block):
    return block * lax.rsqrt(jnp.mean(block * block, axis=-1, keepdims=True) + 1e-06)


def tail_body(k_ref, v_ref, z_ref):
    z_ref[...] = (k_ref[...].astype(jnp.float32) * v_ref[...].astype(jnp.float32)).astype(jnp.bfloat16)


def last_products(keys, values, taps):
    rows, chans = keys.shape
    at = rows // taps - 1
    spec = pl.BlockSpec((taps, chans), lambda i: (at, 0))
    return pl.pallas_call(
        tail_body,
        grid=(1,),
        out_shape=jax.ShapeDtypeStruct((taps, chans), jnp.bfloat16),
        in_specs=[spec, spec],
        out_specs=pl.BlockSpec((taps, chans), lambda i: (0, 0)),
        name="last_products",
    )(keys, values)


def mix_body(g_ref, k_ref, v_ref, e_ref, f_ref, fwd_ref, short_ref, inv_ref, o_ref, ext):
    rows, wide = g_ref.shape
    taps = f_ref.shape[1]
    filt = f_ref[...]
    high = filt.astype(jnp.bfloat16)
    low = (filt - high.astype(jnp.float32)).astype(jnp.bfloat16)
    fhat = lax.dot_general(
        short_ref[...], jnp.concatenate([high, low], 1), (((1,), (1,)), ((), ())),
        preferred_element_type=jnp.float32,
    )
    fc, fs = fhat[:taps], fhat[taps:]
    ext[:taps] = e_ref[...]
    ext[taps:] = (k_ref[...].astype(jnp.float32) * v_ref[...].astype(jnp.float32)).astype(jnp.bfloat16)
    for b in range(rows // taps):
        zhat = jnp.dot(fwd_ref[...], ext[b * taps:(b + 2) * taps], preferred_element_type=jnp.float32)
        zc, zs = zhat[:taps], zhat[taps:]
        prod = jnp.concatenate(
            [(fc * zc - fs * zs).astype(jnp.bfloat16), (fc * zs + fs * zc).astype(jnp.bfloat16)], 0
        )
        mixed = jnp.dot(inv_ref[...], prod, preferred_element_type=jnp.float32)
        here = slice(b * taps, (b + 1) * taps)
        o_ref[here] = (g_ref[here].astype(jnp.float32) * mixed).astype(jnp.bfloat16)


def mix(gate, keys, values, earlier, filters):
    rows, chans = gate.shape
    taps = filters.shape[1]
    wide = 256
    fwd, short, inv = transforms(taps)
    stream = pl.BlockSpec((rows, wide), lambda c: (0, c))
    fixed = lambda a: pl.BlockSpec(a.shape, lambda c: (0, 0))
    return pl.pallas_call(
        mix_body,
        grid=(chans // wide,),
        out_shape=jax.ShapeDtypeStruct((rows, chans), jnp.bfloat16),
        in_specs=[
            stream, stream, stream,
            pl.BlockSpec((taps, wide), lambda c: (0, c)),
            pl.BlockSpec((wide, taps), lambda c: (c, 0)),
            fixed(fwd), fixed(short), fixed(inv),
        ],
        out_specs=stream,
        scratch_shapes=[pltpu.VMEM((rows + taps, wide), jnp.bfloat16)],
        cost_estimate=pl.CostEstimate(
            flops=chans * rows * taps * 14, bytes_accessed=chans * rows * 10, transcendentals=0
        ),
        name="mix",
    )(gate, keys, values, earlier, filters, fwd, short, inv)


def dispatch_body(idx_ref, a_ref, b_ref, c_ref, d_ref, oa_ref, ob_ref, oc_ref, od_ref):
    def norm(src, dst):
        for h in range(dst.shape[1] // HEAD_DIM):
            at = slice(h * HEAD_DIM, (h + 1) * HEAD_DIM)
            dst[:, at] = unit(src[0, :, at].astype(jnp.float32)).astype(jnp.bfloat16)

    norm(a_ref, oa_ref)
    norm(b_ref, ob_ref)

    @pl.when(pl.program_id(0) == 0)
    def _():
        norm(c_ref, oc_ref)
        norm(d_ref, od_ref)


def dispatch(idx, queries, count):
    windows, toks, chans = queries.shape
    source = lambda at: pl.BlockSpec((1, toks, chans), lambda g, i: (i[at(g)], 0, 0))
    moving = pl.BlockSpec((toks, chans), lambda g, i: (g, 0))
    still = pl.BlockSpec((toks, chans), lambda g, i: (0, 0))
    big = jax.ShapeDtypeStruct((count * toks, chans), jnp.bfloat16)
    small = jax.ShapeDtypeStruct((toks, chans), jnp.bfloat16)
    return pl.pallas_call(
        dispatch_body,
        grid_spec=pltpu.PrefetchScalarGridSpec(
            num_scalar_prefetch=1,
            grid=(count,),
            in_specs=[
                source(lambda g: g), source(lambda g: count + g),
                source(lambda g: 2 * count), source(lambda g: 2 * count + 1),
            ],
            out_specs=[moving, moving, still, still],
        ),
        out_shape=[big, big, small, small],
        name="dispatch",
    )(idx, queries, queries, queries, queries)


def attend_body(slot, info_ref, temps_ref, q_ref, h_ref, o_ref):
    rows = h_ref.shape[0]
    head = pl.program_id(0)
    heads = q_ref.shape[1] // HEAD_DIM

    def work():
        off = info_ref[slot]
        live = lax.broadcasted_iota(jnp.int32, (rows, HEAD_DIM), 0) < off
        one = jnp.where(live, 1.0, 0.0).astype(jnp.bfloat16)
        for n in range(heads):
            at = slice(n * HEAD_DIM, (n + 1) * HEAD_DIM)
            value = h_ref[:, at].astype(jnp.float32)
            keyed = unit(value).astype(jnp.bfloat16)
            valued = jnp.concatenate([jnp.where(live, value, 0.0).astype(jnp.bfloat16), one], 1)
            scores = lax.dot_general(
                q_ref[:, at], keyed, (((1,), (1,)), ((), ())), preferred_element_type=jnp.float32
            )
            weights = jnp.exp2(scores * (temps_ref[head * heads + n] * (LOG2E / HEAD_DIM)))
            numer = jnp.dot(weights.astype(jnp.bfloat16), valued, preferred_element_type=jnp.float32)
            o_ref[:, at] = (numer[:, :HEAD_DIM] / numer[:, HEAD_DIM:]).astype(jnp.bfloat16)

    if slot < 2:
        work()
    else:
        @pl.when(info_ref[4] == 1)
        def _():
            work()

        @pl.when(info_ref[4] == 0)
        def _():
            o_ref[...] = jnp.zeros_like(o_ref)


def attend(slot, info, temps, q, hyena):
    toks, chans = q.shape
    rows = hyena.shape[0]
    wide = 2 * HEAD_DIM
    return pl.pallas_call(
        functools.partial(attend_body, slot),
        grid=(chans // wide,),
        out_shape=jax.ShapeDtypeStruct((toks, chans), jnp.bfloat16),
        in_specs=[
            pl.BlockSpec(memory_space=pltpu.SMEM),
            pl.BlockSpec(memory_space=pltpu.SMEM),
            pl.BlockSpec((toks, wide), lambda c: (0, c)),
            pl.BlockSpec((rows, wide), lambda c: (0, c)),
        ],
        out_specs=pl.BlockSpec((toks, wide), lambda c: (0, c)),
        cost_estimate=pl.CostEstimate(
            flops=6 * toks * rows * chans,
            bytes_accessed=2 * chans * (2 * toks + rows),
            transcendentals=toks * rows * chans // HEAD_DIM,
        ),
        name=f"attend{slot}",
    )(info, temps, q, hyena)


def combine_body(blocks_ref, within_ref, a_ref, b_ref, c_ref, d_ref, o_ref):
    at = within_ref[pl.program_id(0)]
    for slot, ref in enumerate((a_ref, b_ref, c_ref, d_ref)):
        @pl.when(at == slot)
        def _(ref=ref):
            o_ref[0] = ref[...]


def combine(blocks, within, parts, windows):
    toks, chans = parts[2].shape
    moving = pl.BlockSpec((toks, chans), lambda w, b, s: (b[w], 0))
    still = pl.BlockSpec((toks, chans), lambda w, b, s: (0, 0))
    return pl.pallas_call(
        combine_body,
        grid_spec=pltpu.PrefetchScalarGridSpec(
            num_scalar_prefetch=2,
            grid=(windows,),
            in_specs=[moving, moving, still, still],
            out_specs=pl.BlockSpec((1, toks, chans), lambda w, b, s: (w, 0, 0)),
        ),
        out_shape=jax.ShapeDtypeStruct((windows, toks, chans), jnp.bfloat16),
        name="combine",
    )(blocks, within, *parts)


def shards(gate_stream, key_stream, value_stream, filters, temps, queries, blocks, sites):
    rows, chans = gate_stream.shape
    taps = filters.shape[1]
    count = lax.axis_size("pos")
    me = lax.axis_index("pos")
    windows = blocks.shape[0]

    order = jnp.arange(windows, dtype=jnp.int32)
    same = (blocks[:, None] == blocks[None, :]) & (order[None, :] < order[:, None])
    within = jnp.sum(same, axis=1, dtype=jnp.int32)
    target = jnp.concatenate(
        [jnp.arange(2 * count, dtype=jnp.int32), jnp.full((2,), 2 * count, jnp.int32)
         + jnp.arange(2, dtype=jnp.int32)]
    )
    place = jnp.where(within < 2, within * count + blocks, 2 * count + within - 2)
    hit = place[None, :] == target[:, None]
    idx = jnp.sum(jnp.where(hit, order[None, :], 0), axis=1, dtype=jnp.int32)
    slots = jnp.arange(4, dtype=jnp.int32)
    mine = (blocks == me)[None, :] & (within[None, :] == slots[:, None])
    found = jnp.sum(mine, axis=1, dtype=jnp.int32)
    offsets = jnp.sum(jnp.where(mine, sites[None, :] - me * rows, 0), axis=1, dtype=jnp.int32)
    offsets = jnp.where(found > 0, offsets, rows)
    info = jnp.concatenate([offsets, found[2:3]])

    tail = last_products(key_stream, value_stream, taps)
    earlier = lax.ppermute(tail, "pos", [(i, i + 1) for i in range(count - 1)])
    sent = dispatch(idx, queries, count)
    got0 = lax.all_to_all(sent[0], "pos", 0, 0, tiled=True)
    got1 = lax.all_to_all(sent[1], "pos", 0, 0, tiled=True)
    got2 = lax.all_gather(sent[2], "pos", axis=0, tiled=True)
    got3 = lax.all_gather(sent[3], "pos", axis=0, tiled=True)
    hyena_out = mix(gate_stream, key_stream, value_stream, earlier, filters)
    back0 = lax.all_to_all(attend(0, info, temps, got0, hyena_out), "pos", 0, 0, tiled=True)
    back1 = lax.all_to_all(attend(1, info, temps, got1, hyena_out), "pos", 0, 0, tiled=True)
    back2 = lax.psum_scatter(
        attend(2, info, temps, got2, hyena_out), "pos", scatter_dimension=0, tiled=True
    )
    back3 = lax.psum_scatter(
        attend(3, info, temps, got3, hyena_out), "pos", scatter_dimension=0, tiled=True
    )
    attended = combine(blocks, within, (back0, back1, back2, back3), windows)
    return (hyena_out, attended)


def solution(mesh):
    placed = (
        P(("groups", "pos"), "mp"),
        P(("groups", "pos"), "mp"),
        P(("groups", "pos"), "mp"),
        P("mp", None),
        P("mp"),
        P("groups", "pos", "mp"),
        P("groups"),
        P("groups"),
    )
    return jax.shard_map(
        shards,
        mesh=mesh,
        in_specs=placed,
        out_specs=(P(("groups", "pos"), "mp"), P("groups", "pos", "mp")),
        check_vma=False,
    )
```

time: 293 us -> 282 us (0.962)
  waiting for transfers between devices: 19.8 us -> 140 us
  matrix products: 70.8 us -> 0 us
  local copies, waits for them, and re-layouts: 65.1 us -> 1.51 us
  blocking collectives: 96.9 us -> 34.3 us
  Pallas kernels: 0 us -> 59.8 us
  other arithmetic: 27.7 us -> 3.64 us
  starting transfers between devices: 9.21 us -> 25.4 us
  between operations: 0.82 us -> 13.8 us
    reduce_scatter x0 -> x2, waiting for transfers between devices: none -> 65 us  [the longest x1 65 us: shards(): lax.psum_scatter(attend(3, info, temps, got3, hyena_out), 'pos', scatter_...]
    all_to_all x1, blocking collectives: 96.9 us -> 34.3 us  [shards(): lax.all_to_all(attend(0, info, temps, got0, hyena_out), 'pos', 0, 0, tile...]
    pallas_call x0 -> x8, Pallas kernels: none -> 59.8 us  [the longest x4 28.4 us: attend(): pl.pallas_call(functools.partial(attend_body, slot), grid=(chans // wide,...]
    conv_general_dilated x1 -> x0, matrix products: 45.5 us -> none  [causal_mix(): lax.conv_general_dilated(extended.astype(jnp.float32)[None], kernel, (1,)...]
    all_to_all x1 -> x3, waiting for transfers between devices: 19.8 us -> 49.3 us  [the longest x1 31.8 us: shards(): got1 = lax.all_to_all(sent[1], 'pos', 0, 0, tiled=True)]
    dot_general x10 -> x0, matrix products: 25.4 us -> none  [the longest x4 14.5 us: attend_slot(): jnp.einsum('qhd,khd->hqk', qnorm, keyed, preferred_element_type=jnp.float32)]
    ppermute x1, waiting for transfers between devices: 0.01 us -> 24.9 us  [shards(): earlier = lax.ppermute(tail, 'pos', [(i, i + 1) for i in range(count - 1)])]
    while x15 -> x0, local copies, waits for them, and re-layouts: 18.5 us -> none  [the longest x3 16.9 us: shards(): results = lax.map(one_slot, (arrived, offsets))]
  transfers between devices with their start and end apart: 2 -> 8, of which waited for: 1 -> 4; matrix products, arithmetic and copies ran while one was open for 32% -> 1% of each run, Pallas kernels for 0% -> 15%
where the time goes in v1:
time: 282 us; the launch traced here: 278 us
  waiting for transfers between devices  140 us (50%)
  Pallas kernels  59.8 us (21%)
  blocking collectives  34.3 us (12%)
  starting transfers between devices  25.4 us (9%)
  between operations  13.8 us (5%)
  other arithmetic  3.64 us (1%)
    reduce_scatter x1, waiting for transfers between devices, shards(): lax.psum_scatter(attend(3, info, temps, got3, hyena_out), 'pos', scatter_...  65 us
    all_to_all x1, blocking collectives, shards(): lax.all_to_all(attend(0, info, temps, got0, hyena_out), 'pos', 0, 0, tile...  34.3 us
    all_to_all x1, waiting for transfers between devices, shards(): got1 = lax.all_to_all(sent[1], 'pos', 0, 0, tiled=True)  31.8 us
    pallas_call x4, Pallas kernels, attend(): pl.pallas_call(functools.partial(attend_body, slot), grid=(chans // wide,...  28.4 us
    ppermute x1, waiting for transfers between devices, shards(): earlier = lax.ppermute(tail, 'pos', [(i, i + 1) for i in range(count - 1)])  24.9 us
    all_to_all x1, waiting for transfers between devices, shards(): lax.all_to_all(attend(1, info, temps, got1, hyena_out), 'pos', 0, 0, tile...  17.4 us
    all_to_all x1, starting transfers between devices, shards(): lax.all_to_all(attend(1, info, temps, got1, hyena_out), 'pos', 0, 0, tile...  11.5 us
    pallas_call x1, Pallas kernels, mix(): pl.pallas_call(mix_body, grid=(chans // wide,), out_shape=jax.ShapeDtypeS...  11 us
  transfers between devices with their start and end apart: 8, of which 4 were waited for; matrix products, arithmetic and copies ran while one was open for 1% of the time, Pallas kernels for 15%

profile of v1, /device:TPU:6, one launch (start us, length us, event | category | flops | bytes accessed | tf_op | source)
XLA Modules:
  0.0 278.3 jit_solution(5143340239194310408)
XLA Ops:
  7.2 0.0 all-gather.3.cloned.1.call-start
  7.2 0.9 convert_reduce_fusion.within_ref
  8.1 0.0 copy-start.4
  8.1 0.7 compare_select_fusion
  8.8 0.1 pad_add_fusion.1
  8.9 0.6 select_reduce_fusion.idx_ref
  9.5 7.6 %dispatch.1 = (bf16[256,2048]{1,0:T(8,128)(2,1)}, bf16[256,2048]{1,0:T(8,128)(2,1)}, bf16[32,2048]{1,0:T(8,128)(2,1)}, bf16[32,2048]{1,0:T(8,128)(2,1)}) custom-call(s32[18]{0:T(128)} %select_reduce_fusion.idx_ref, bf16[16,32,2048]{2,1,0:T(8,128)(2,1)} %d_ref.1, bf16[16,32,2048]{2,1,0:T(8,128)(2,1)} %d_ref.1, bf16[16,32,2048]{2,1,0:T(8,128)(2,1)} %d_ref.1, ...), custom_call_target="tpu_custom_call" | custom-call | tf_op jit(solution)/shard_map/dispatch/pallas_call | solution.py:122
  17.1 0.0 all-gather.3.cloned.1.call-update
  17.1 6.3 %all-to-all-start.2 = ((bf16[8,32,2048]{2,1,0:T(8,128)(2,1)}), bf16[8,32,2048]{2,1,0:T(8,128)(2,1)S(1)}, u32[]{:S(2)}, u32[]{:S(2)}) async-start(bf16[8,32,2048]{2,1,0:T(8,128)(2,1)} %bitcast.13), calls=%async_computation.2 | async-start | bytes 2097152 | tf_op jit(solution)/shard_map/all_to_all | solution.py:248
  23.4 0.0 all-gather.5.cloned.1.call-start
  23.5 0.7 all-gather.5.cloned.1.call-update
  24.2 31.8 %all-to-all-done.2 = bf16[8,32,2048]{2,1,0:T(8,128)(2,1)S(1)} async-done(((bf16[8,32,2048]{2,1,0:T(8,128)(2,1)}), bf16[8,32,2048]{2,1,0:T(8,128)(2,1)S(1)}, u32[]{:S(2)}, u32[]{:S(2)}) %all-to-all-start.2) | async-done | bytes 1048608 | tf_op jit(solution)/shard_map/all_to_all | solution.py:248
  56.0 0.0 copy-start.2
  56.0 4.1 %all-to-all-start = ((bf16[8,32,2048]{2,1,0:T(8,128)(2,1)}), bf16[8,32,2048]{2,1,0:T(8,128)(2,1)S(1)}, u32[]{:S(2)}, u32[]{:S(2)}) async-start(bf16[8,32,2048]{2,1,0:T(8,128)(2,1)} %bitcast), calls=%async_computation | async-start | bytes 2097152 | tf_op jit(solution)/shard_map/all_to_all | solution.py:247
  60.2 0.0 copy-start.5
  60.2 0.0 copy-start.6
  60.2 0.0 reduce-scatter.3.cloned.1.call-start
  60.2 2.1 last_products.1
  62.3 0.0 copy-done.2
  62.3 3.4 %collective-permute-start = (bf16[128,2048]{1,0:T(8,128)(2,1)}, bf16[128,2048]{1,0:T(8,128)(2,1)S(1)}, u32[]{:S(2)}, u32[]{:S(2)}) collective-permute-start(bf16[128,2048]{1,0:T(8,128)(2,1)} %last_products.1), channel_id=1, source_target_pairs={{0,2},{2,4},{4,6},{6,8},{8,10},{10,12},{12,14},{1,3},{3,5},{5,7},{... | collective-permute-start | bytes 1572872 | tf_op jit(solution)/shard_map/ppermute | solution.py:245
  65.7 0.0 copy-done.5
  65.7 0.0 copy-done.6
  65.7 0.0 copy-done.4
  65.8 0.1 select_reduce_fusion.1
  65.9 0.6 slice.3
  66.6 1.2 pad_add_fusion.info_ref
  67.8 24.9 %collective-permute-done.e_ref = bf16[128,2048]{1,0:T(8,128)(2,1)S(1)} collective-permute-done((bf16[128,2048]{1,0:T(8,128)(2,1)}, bf16[128,2048]{1,0:T(8,128)(2,1)S(1)}, u32[]{:S(2)}, u32[]{:S(2)}) %collective-permute-start) | collective-permute-done | bytes 524320 | tf_op jit(solution)/shard_map/ppermute | solution.py:245
  92.6 0.0 copy-start.3
  92.6 0.8 copy-done.3
  93.5 11.0 %mix.1.h_ref = bf16[512,2048]{1,0:T(8,128)(2,1)} custom-call(bf16[512,2048]{1,0:T(8,128)(2,1)} %g_ref.1, bf16[512,2048]{1,0:T(8,128)(2,1)} %k_ref.3, bf16[512,2048]{1,0:T(8,128)(2,1)} %v_ref.3, bf16[128,2048]{1,0:T(8,128)(2,1)} %copy-done.3, f32[2048,128]{1,0:T(8,128)} %f_ref.1, bf16[256,256]{1,0:T(8,128)(2,1)} %constant.27.clone.fwd_ref, ...), custom_call_target="tpu_custom_call" | custom-call | flops 1879048192 | bytes 10485760 | tf_op jit(solution)/shard_map/mix/pallas_call | solution.py:81
  104.5 0.0 all-gather.3.cloned.1.call-done.q_ref
  104.5 5.8 %attend2.1 = bf16[256,2048]{1,0:T(8,128)(2,1)} custom-call(s32[5]{0:T(128)} %pad_add_fusion.info_ref, f32[16]{0:T(128)} %temps_ref.7, bf16[256,2048]{1,0:T(8,128)(2,1)} %all-gather.3.cloned.1.call-done.q_ref, bf16[512,2048]{1,0:T(8,128)(2,1)} %mix.1.h_ref), custom_call_target="tpu_custom_call" | custom-call | flops 1610612736 | bytes 4194304 | tf_op jit(solution)/shard_map/attend2/pallas_call | solution.py:175
  110.3 0.0 reduce-scatter.3.cloned.1.call-update
  110.4 8.3 %attend1.1 = bf16[256,2048]{1,0:T(8,128)(2,1)} custom-call(s32[5]{0:T(128)} %pad_add_fusion.info_ref, f32[16]{0:T(128)} %temps_ref.7, bf16[256,2048]{1,0:T(8,128)(2,1)} %bitcast.11, bf16[512,2048]{1,0:T(8,128)(2,1)} %mix.1.h_ref), custom_call_target="tpu_custom_call" | custom-call | flops 1610612736 | bytes 4194304 | tf_op jit(solution)/shard_map/attend1/pallas_call | solution.py:175
  118.7 0.0 all-to-all-done
  118.7 0.0 copy-start.1
  118.7 11.5 %all-to-all-start.3 = ((bf16[8,32,2048]{2,1,0:T(8,128)(2,1)}), bf16[8,32,2048]{2,1,0:T(8,128)(2,1)S(1)}, u32[]{:S(2)}, u32[]{:S(2)}) async-start(bf16[8,32,2048]{2,1,0:T(8,128)(2,1)} %bitcast.12), calls=%async_computation.3 | async-start | bytes 2097152 | tf_op jit(solution)/shard_map/all_to_all | solution.py:253
  130.2 0.0 reduce-scatter.5.cloned.1.call-start
  130.2 0.0 all-gather.5.cloned.1.call-done.q_ref
  130.2 5.8 %attend3.1 = bf16[256,2048]{1,0:T(8,128)(2,1)} custom-call(s32[5]{0:T(128)} %pad_add_fusion.info_ref, f32[16]{0:T(128)} %temps_ref.7, bf16[256,2048]{1,0:T(8,128)(2,1)} %all-gather.5.cloned.1.call-done.q_ref, bf16[512,2048]{1,0:T(8,128)(2,1)} %mix.1.h_ref), custom_call_target="tpu_custom_call" | custom-call | flops 1610612736 | bytes 4194304 | tf_op jit(solution)/shard_map/attend3/pallas_call | solution.py:175
  136.0 0.0 copy-done.1
  136.0 0.0 reduce-scatter.5.cloned.1.call-update
  136.1 8.3 %attend0.1 = bf16[256,2048]{1,0:T(8,128)(2,1)} custom-call(s32[5]{0:T(128)} %pad_add_fusion.info_ref, f32[16]{0:T(128)} %temps_ref.7, bf16[256,2048]{1,0:T(8,128)(2,1)} %bitcast.10, bf16[512,2048]{1,0:T(8,128)(2,1)} %mix.1.h_ref), custom_call_target="tpu_custom_call" | custom-call | flops 1610612736 | bytes 4194304 | tf_op jit(solution)/shard_map/attend0/pallas_call | solution.py:175
  144.4 17.4 %all-to-all-done.3 = bf16[8,32,2048]{2,1,0:T(8,128)(2,1)S(1)} async-done(((bf16[8,32,2048]{2,1,0:T(8,128)(2,1)}), bf16[8,32,2048]{2,1,0:T(8,128)(2,1)S(1)}, u32[]{:S(2)}, u32[]{:S(2)}) %all-to-all-start.3) | async-done | bytes 1048608 | tf_op jit(solution)/shard_map/all_to_all | solution.py:253
  161.8 0.0 copy-start
  161.8 34.3 %all_to_all.44 = bf16[8,32,2048]{2,1,0:T(8,128)(2,1)} all-to-all(bf16[8,32,2048]{2,1,0:T(8,128)(2,1)} %bitcast.14), channel_id=1, replica_groups=mesh['groups'=2,'pos'=8,'mp'=2] {'pos'}, dimensions={0} | all-to-all | bytes 2097152 | tf_op jit(solution)/shard_map/all_to_all | solution.py:252
  196.1 0.0 reduce-scatter.3.cloned.1.call-done.c_ref
  196.1 65.0 %reduce-scatter.5.cloned.1.call-done.d_ref = bf16[32,2048]{1,0:T(8,128)(2,1)} async-done(((bf16[256,2048]{1,0:T(8,128)(2,1)}), bf16[32,2048]{1,0:T(8,128)(2,1)}) %reduce-scatter.5.cloned.1.call-update) | async-done | bytes 131088 | tf_op jit(solution)/shard_map/reduce_scatter | solution.py:257
  261.1 0.0 copy-done
  261.1 10.7 %combine.1 = bf16[16,32,2048]{2,1,0:T(8,128)(2,1)} custom-call(s32[16]{0:T(128)} %blocks_ref.1, s32[16]{0:T(128)} %copy-done.4, bf16[256,2048]{1,0:T(8,128)(2,1)} %bitcast.9, bf16[256,2048]{1,0:T(8,128)(2,1)} %bitcast.8, bf16[32,2048]{1,0:T(8,128)(2,1)} %reduce-scatter.3.cloned.1.call-done.c_ref, bf16[32,2048]{1,0:T(8,128)(2,1)} %reduce-scatter.5.cloned.1.call-done.d_ref), custom_call_target="tpu_custom_call" | custom-call | tf_op jit(solution)/shard_map/combine/pallas_call | solution.py:207
  (5 shorter events, 0.0 us)
Async XLA Ops:
  7.2 97.4 %all-gather.3.cloned.1.call-start = ((), (), s32[]{:S(2)}) async-start(), calls=%async_computation.6 | async-start | bytes 1179648 | tf_op jit(solution)/shard_map/all_gather | solution.py:249
  8.1 57.6 %copy-start.4 = (s32[16]{0:T(128)}, s32[16]{0:T(128)S(1)}, u32[]{:S(2)}) copy-start(s32[16]{0:T(128)S(1)} %convert_reduce_fusion.within_ref) | copy-start | bytes 196
  17.1 38.9 %all-to-all-start.2 = ((bf16[8,32,2048]{2,1,0:T(8,128)(2,1)}), bf16[8,32,2048]{2,1,0:T(8,128)(2,1)S(1)}, u32[]{:S(2)}, u32[]{:S(2)}) async-start(bf16[8,32,2048]{2,1,0:T(8,128)(2,1)} %bitcast.13), calls=%async_computation.2 | async-start | bytes 2097152 | tf_op jit(solution)/shard_map/all_to_all | solution.py:248
  23.4 106.7 %all-gather.5.cloned.1.call-start = ((), (), s32[]{:S(2)}) async-start(), calls=%async_computation.8 | async-start | bytes 1179648 | tf_op jit(solution)/shard_map/all_gather | solution.py:250
  56.0 6.3 %copy-start.2 = (bf16[8,32,2048]{2,1,0:T(8,128)(2,1)}, bf16[8,32,2048]{2,1,0:T(8,128)(2,1)S(1)}, u32[]{:S(2)}) copy-start(bf16[8,32,2048]{2,1,0:T(8,128)(2,1)S(1)} %all-to-all-done.2) | copy-start | bytes 3145732
  56.0 62.7 %all-to-all-start = ((bf16[8,32,2048]{2,1,0:T(8,128)(2,1)}), bf16[8,32,2048]{2,1,0:T(8,128)(2,1)S(1)}, u32[]{:S(2)}, u32[]{:S(2)}) async-start(bf16[8,32,2048]{2,1,0:T(8,128)(2,1)} %bitcast), calls=%async_computation | async-start | bytes 2097152 | tf_op jit(solution)/shard_map/all_to_all | solution.py:247
  60.2 5.5 %copy-start.5 = (s32[16]{0:T(128)S(1)}, s32[16]{0:T(128)}, u32[]{:S(2)}) copy-start(s32[16]{0:T(128)} %blocks_ref.1) | copy-start | bytes 196
  60.2 5.6 %copy-start.6 = (s32[16]{0:T(128)S(1)}, s32[16]{0:T(128)}, u32[]{:S(2)}) copy-start(s32[16]{0:T(128)} %param.18) | copy-start | bytes 196
  60.2 135.9 %reduce-scatter.3.cloned.1.call-start = ((), (), s32[]{:S(2)}) async-start(), calls=%async_computation.7 | async-start | bytes 1179648 | tf_op jit(solution)/shard_map/reduce_scatter | solution.py:254
  62.3 30.3 %collective-permute-start = (bf16[128,2048]{1,0:T(8,128)(2,1)}, bf16[128,2048]{1,0:T(8,128)(2,1)S(1)}, u32[]{:S(2)}, u32[]{:S(2)}) collective-permute-start(bf16[128,2048]{1,0:T(8,128)(2,1)} %last_products.1), channel_id=1, source_target_pairs={{0,2},{2,4},{4,6},{6,8},{8,10},{10,12},{12,14},{1,3},{3,5},{5,7},{... | collective-permute-start | bytes 1572872 | tf_op jit(solution)/shard_map/ppermute | solution.py:245
  92.6 0.8 copy-start.3
  118.7 17.3 %copy-start.1 = (bf16[8,32,2048]{2,1,0:T(8,128)(2,1)}, bf16[8,32,2048]{2,1,0:T(8,128)(2,1)S(1)}, u32[]{:S(2)}) copy-start(bf16[8,32,2048]{2,1,0:T(8,128)(2,1)S(1)} %all-to-all-done) | copy-start | bytes 3145732
  118.7 43.1 %all-to-all-start.3 = ((bf16[8,32,2048]{2,1,0:T(8,128)(2,1)}), bf16[8,32,2048]{2,1,0:T(8,128)(2,1)S(1)}, u32[]{:S(2)}, u32[]{:S(2)}) async-start(bf16[8,32,2048]{2,1,0:T(8,128)(2,1)} %bitcast.12), calls=%async_computation.3 | async-start | bytes 2097152 | tf_op jit(solution)/shard_map/all_to_all | solution.py:253
  130.2 130.9 %reduce-scatter.5.cloned.1.call-start = ((), (), s32[]{:S(2)}) async-start(), calls=%async_computation.9 | async-start | bytes 1179648 | tf_op jit(solution)/shard_map/reduce_scatter | solution.py:257
  161.8 99.2 %copy-start = (bf16[8,32,2048]{2,1,0:T(8,128)(2,1)}, bf16[8,32,2048]{2,1,0:T(8,128)(2,1)S(1)}, u32[]{:S(2)}) copy-start(bf16[8,32,2048]{2,1,0:T(8,128)(2,1)S(1)} %all-to-all-done.3) | copy-start | bytes 3145732
Sparse Core Ops, SparseCore 0:
  17.2 47.9 all-gather.2
  67.4 48.0 all-gather.4
  118.9 75.6 reduce-scatter.2
  197.9 63.1 reduce-scatter.4

commit v2 on v1

v2 whole, which is shorter than its diff:
```python
import functools
import math

import jax
import jax.numpy as jnp
import numpy as np
from jax import lax
from jax.experimental import pallas as pl
from jax.experimental.pallas import tpu as pltpu
from jax.sharding import PartitionSpec as P

HEAD_DIM = 128
LOG2E = math.log2(math.e)


def transforms(taps):
    size = 2 * taps
    freq = (np.arange(taps) + 0.5) * (2 * np.pi / size)
    grid = freq[:, None] * np.arange(size)[None, :]
    both = np.concatenate([np.cos(grid), np.sin(grid)], 0)
    forward = both / size
    short = both[:, :taps] / taps
    inverse = both[:, taps:].T * taps * 2.0
    cast = lambda a: jnp.asarray(a, jnp.bfloat16)
    return cast(forward), cast(np.concatenate([short, short], 1)), cast(inverse)


def unit(block):
    return block * lax.rsqrt(jnp.mean(block * block, axis=-1, keepdims=True) + 1e-06)


def dispatch_body(idx_ref, a_ref, b_ref, c_ref, d_ref, oa_ref, ob_ref, ox_ref):
    toks = a_ref.shape[1]

    def norm(src, dst, first):
        for h in range(dst.shape[-1] // HEAD_DIM):
            at = slice(h * HEAD_DIM, (h + 1) * HEAD_DIM)
            dst[first, at] = unit(src[0, :, at].astype(jnp.float32)).astype(jnp.bfloat16)

    norm(a_ref, oa_ref.at[0], slice(0, toks))
    norm(b_ref, ob_ref.at[0], slice(0, toks))

    @pl.when(pl.program_id(0) == 0)
    def _():
        norm(c_ref, ox_ref, slice(0, toks))
        norm(d_ref, ox_ref, slice(toks, 2 * toks))


def dispatch(idx, queries, count):
    windows, toks, chans = queries.shape
    source = lambda at: pl.BlockSpec((1, toks, chans), lambda g, i: (i[at(g)], 0, 0))
    moving = pl.BlockSpec((1, toks, chans), lambda g, i: (g, 0, 0))
    still = pl.BlockSpec((2 * toks, chans), lambda g, i: (0, 0))
    big = jax.ShapeDtypeStruct((count, toks, chans), jnp.bfloat16)
    small = jax.ShapeDtypeStruct((2 * toks, chans), jnp.bfloat16)
    return pl.pallas_call(
        dispatch_body,
        grid_spec=pltpu.PrefetchScalarGridSpec(
            num_scalar_prefetch=1,
            grid=(count,),
            in_specs=[
                source(lambda g: g), source(lambda g: count + g),
                source(lambda g: 2 * count), source(lambda g: 2 * count + 1),
            ],
            out_specs=[moving, moving, still],
        ),
        out_shape=[big, big, small],
        name="dispatch",
    )(idx, queries, queries, queries, queries)


def fused_body(
    n, inner, info_ref, temps_ref, fwd_ref, short_ref, inv_ref, g_hbm, k_hbm, v_hbm, f_hbm,
    d0_hbm, d1_hbm, e_hbm, hyena_out, back0, back1, backx,
    gv, kv, vv, fv, tail, halo, hy, keyed, q0, q1, qx, o0, o1, ox, acc, side, rise, fall, last,
    load, local, halo_sem, go_send, go_recv, ret_send, ret_recv, up_send, up_recv,
    down_send, down_recv, part_send, part_recv, rpart_send, rpart_recv,
    rup_send, rup_recv, rdown_send, rdown_recv,
):
    outer = n // inner
    me = lax.axis_index("pos")
    zi, yi = me // inner, me % inner
    rows, chans = gv.shape
    taps = fv.shape[1]
    toks = q0.shape[1]
    wide = 2 * HEAD_DIM

    def remote(src, dst, send, recv, who):
        return pltpu.make_async_remote_copy(
            src_ref=src, dst_ref=dst, send_sem=send, recv_sem=recv,
            device_id={"pos": who}, device_id_type=pl.DeviceIdType.MESH,
        )

    loads = [
        pltpu.make_async_copy(src, dst, load.at[i])
        for i, (src, dst) in enumerate(
            ((k_hbm, kv), (v_hbm, vv), (e_hbm, qx.at[me]), (g_hbm, gv), (f_hbm, fv))
        )
    ]
    for copy in loads:
        copy.start()
    own = [
        pltpu.make_async_copy(d0_hbm.at[me], q0.at[me], local.at[0]),
        pltpu.make_async_copy(d1_hbm.at[me], q1.at[me], local.at[1]),
    ]
    for copy in own:
        copy.start()

    barrier = pltpu.get_barrier_semaphore()
    for off in range(1, n):
        pl.semaphore_signal(
            barrier, inc=1, device_id={"pos": (me + off) % n}, device_id_type=pl.DeviceIdType.MESH
        )
    pl.semaphore_wait(barrier, n - 1)

    loads[0].wait()
    loads[1].wait()
    at = slice(rows - taps, rows)
    tail[...] = (kv[at].astype(jnp.float32) * vv[at].astype(jnp.float32)).astype(jnp.bfloat16)
    halo_copy = remote(tail, halo, halo_sem.at[0], halo_sem.at[1], (me + 1) % n)

    @pl.when(me < n - 1)
    def _():
        halo_copy.start()

    loads[2].wait()

    def across(z):
        slot = z * inner + yi
        return remote(
            qx.at[slot], qx.at[slot], part_send.at[z], part_recv.at[z], zi * inner + (inner - 1 - yi)
        )

    def upward(step):
        slot = jnp.maximum(zi - step + 1, 0) * inner + yi
        to = jnp.minimum(zi + 1, outer - 1) * inner + yi
        return remote(qx.at[slot], qx.at[slot], up_send.at[step], up_recv.at[step], to)

    def downward(step):
        slot = jnp.minimum(zi + step - 1, outer - 1) * inner + yi
        to = jnp.maximum(zi - 1, 0) * inner + yi
        return remote(qx.at[slot], qx.at[slot], down_send.at[step], down_recv.at[step], to)

    def gather_send(step):
        @pl.when((zi >= step - 1) & (zi < outer - 1))
        def _():
            upward(step).start()

        @pl.when((zi + step - 1 < outer) & (zi > 0))
        def _():
            downward(step).start()

        if inner == 2:
            @pl.when(zi >= step - 1)
            def _():
                across(jnp.maximum(zi - step + 1, 0)).start()

            if step > 1:
                @pl.when(zi + step - 1 < outer)
                def _():
                    across(jnp.minimum(zi + step - 1, outer - 1)).start()

    def gather_recv(step):
        @pl.when(zi >= step)
        def _():
            upward(step).wait_recv()

        @pl.when(zi + step < outer)
        def _():
            downward(step).wait_recv()

    def out_copy(slot, src, dst, off):
        to = (me + off) % n
        return remote(src.at[to], dst.at[me], go_send.at[slot, off], go_recv.at[slot, off], to)

    def back_copy(slot, src, dst, off):
        to = (me + off) % n
        return remote(src.at[to], dst.at[me], ret_send.at[slot, off], ret_recv.at[slot, off], to)

    gather_send(1)
    for off in range(1, n):
        out_copy(0, d0_hbm, q0, off).start()

    loads[3].wait()
    loads[4].wait()

    @pl.when(me > 0)
    def _():
        halo_copy.wait_recv()

    @pl.when(me == 0)
    def _():
        halo[...] = jnp.zeros_like(halo)

    def mix_tile(c, carry):
        cols = pl.ds(pl.multiple_of(c * wide, wide), wide)
        filt = fv[cols, :]
        high = filt.astype(jnp.bfloat16)
        low = (filt - high.astype(jnp.float32)).astype(jnp.bfloat16)
        fhat = lax.dot_general(
            short_ref[...], jnp.concatenate([high, low], 1), (((1,), (1,)), ((), ())),
            preferred_element_type=jnp.float32,
        )
        fc, fs = fhat[:taps], fhat[taps:]
        before = halo[:, cols]
        for b in range(rows // taps):
            here = slice(b * taps, (b + 1) * taps)
            z = (kv[here, cols].astype(jnp.float32) * vv[here, cols].astype(jnp.float32)).astype(jnp.bfloat16)
            zhat = jnp.dot(
                fwd_ref[...], jnp.concatenate([before, z], 0), preferred_element_type=jnp.float32
            )
            before = z
            zc, zs = zhat[:taps], zhat[taps:]
            prod = jnp.concatenate(
                [(fc * zc - fs * zs).astype(jnp.bfloat16), (fc * zs + fs * zc).astype(jnp.bfloat16)], 0
            )
            mixed = jnp.dot(inv_ref[...], prod, preferred_element_type=jnp.float32)
            out = (gv[here, cols].astype(jnp.float32) * mixed).astype(jnp.bfloat16)
            hy[here, cols] = out
            out = out.astype(jnp.float32)
            keyed[here, cols] = jnp.concatenate(
                [unit(out[:, :HEAD_DIM]), unit(out[:, HEAD_DIM:])], 1
            ).astype(jnp.bfloat16)
        return carry

    tiles = chans // wide
    lax.fori_loop(0, tiles, mix_tile, 0)
    hyena_copy = pltpu.make_async_copy(hy, hyena_out, local.at[2])
    hyena_copy.start()

    for off in range(1, n):
        out_copy(1, d1_hbm, q1, off).start()
    for step in range(1, outer):
        gather_recv(step)
        gather_send(step + 1)

    def attend(slot, q, o, first, hot):
        off = info_ref[slot]
        seen = off * hot

        def one(c, carry):
            place = lax.broadcasted_iota(jnp.int32, (rows, HEAD_DIM), 0)
            ones = jnp.where(place < off, 1.0, 0.0).astype(jnp.bfloat16)
            live = jnp.where(place < seen, 1.0, 0.0).astype(jnp.bfloat16)
            for half in range(2):
                cols = pl.ds(pl.multiple_of(c * wide + half * HEAD_DIM, HEAD_DIM), HEAD_DIM)
                rows_q = q[:, pl.ds(first, toks), cols]
                if toks % 16:
                    rows_q = rows_q.astype(jnp.float32)
                rows_q = rows_q.reshape(n * toks, HEAD_DIM).astype(jnp.bfloat16)
                valued = jnp.concatenate([hy[:, cols] * live, ones], 1)
                scores = lax.dot_general(
                    rows_q, keyed[:, cols], (((1,), (1,)), ((), ())),
                    preferred_element_type=jnp.float32,
                )
                weights = jnp.exp2(scores * (temps_ref[c * 2 + half] * (LOG2E / HEAD_DIM)))
                numer = jnp.dot(
                    weights.astype(jnp.bfloat16), valued, preferred_element_type=jnp.float32
                )
                res = numer[:, :HEAD_DIM] / numer[:, HEAD_DIM:]
                o[:, pl.ds(first, toks), cols] = res.reshape(n, toks, HEAD_DIM).astype(jnp.bfloat16)
            return carry

        lax.fori_loop(0, tiles, one, 0)

    own[0].wait()
    for off in range(1, n):
        out_copy(0, d0_hbm, q0, off).wait_recv()
    attend(0, q0, o0, 0, 1)
    for off in range(1, n):
        back_copy(0, o0, back0, off).start()
    mine0 = pltpu.make_async_copy(o0.at[me], back0.at[me], local.at[3])
    mine0.start()

    if inner == 2:
        for z in range(outer):
            across(z).wait_recv()
    hot = info_ref[4]
    attend(2, qx, ox, 0, hot)
    attend(3, qx, ox, toks, hot)

    def swap(z):
        return remote(
            ox.at[z * inner + (inner - 1 - yi)], side.at[z], rpart_send.at[z], rpart_recv.at[z],
            zi * inner + (inner - 1 - yi),
        )

    if inner == 2:
        for z in range(outer):
            swap(z).start()

    own[1].wait()
    for off in range(1, n):
        out_copy(1, d1_hbm, q1, off).wait_recv()
    attend(1, q1, o1, 0, 1)
    for off in range(1, n):
        back_copy(1, o1, back1, off).start()
    mine1 = pltpu.make_async_copy(o1.at[me], back1.at[me], local.at[4])
    mine1.start()

    def lift(z):
        to = jnp.minimum(zi + 1, outer - 1) * inner + yi
        return remote(acc.at[z], rise.at[z], rup_send.at[z], rup_recv.at[z], to)

    def drop(z):
        to = jnp.maximum(zi - 1, 0) * inner + yi
        return remote(acc.at[z], fall.at[z], rdown_send.at[z], rdown_recv.at[z], to)

    for z in range(outer):
        if inner == 2:
            swap(z).wait_recv()
            acc[z] = ox[z * inner + yi] + side[z]
        else:
            acc[z] = ox[z]

    def reduce_up(z):
        @pl.when(zi < z)
        def _():
            @pl.when(zi > 0)
            def _():
                lift(z).wait_recv()
                acc[z] = acc[z] + rise[z]

            lift(z).start()

    def reduce_down(z):
        @pl.when(zi > z)
        def _():
            @pl.when(zi < outer - 1)
            def _():
                drop(z).wait_recv()
                acc[z] = acc[z] + fall[z]

            drop(z).start()

    for step in range(outer - 1):
        reduce_up(outer - 1 - step)
        reduce_down(step)
    last[...] = acc[zi]

    @pl.when(zi > 0)
    def _():
        lift(zi).wait_recv()
        last[...] = last[...] + rise[zi]

    @pl.when(zi < outer - 1)
    def _():
        drop(zi).wait_recv()
        last[...] = last[...] + fall[zi]

    end = pltpu.make_async_copy(last, backx, local.at[5])
    end.start()

    for off in range(1, n):
        back_copy(0, o0, back0, off).wait_recv()
        back_copy(1, o1, back1, off).wait_recv()
    for off in range(1, n):
        out_copy(0, d0_hbm, q0, off).wait_send()
        out_copy(1, d1_hbm, q1, off).wait_send()
        back_copy(0, o0, back0, off).wait_send()
        back_copy(1, o1, back1, off).wait_send()

    @pl.when(me < n - 1)
    def _():
        halo_copy.wait_send()

    for step in range(1, outer):
        @pl.when((zi >= step - 1) & (zi < outer - 1))
        def _(step=step):
            upward(step).wait_send()

        @pl.when((zi + step - 1 < outer) & (zi > 0))
        def _(step=step):
            downward(step).wait_send()

    for z in range(outer):
        if inner == 2:
            across(z).wait_send()
            swap(z).wait_send()

        @pl.when(zi < z)
        def _(z=z):
            lift(z).wait_send()

        @pl.when(zi > z)
        def _(z=z):
            drop(z).wait_send()

    for copy in (hyena_copy, mine0, mine1, end):
        copy.wait()


def fused(info, temps, streams, filters, sent):
    gate, keys, values = streams
    rows, chans = gate.shape
    taps = filters.shape[1]
    n, toks, _ = sent[0].shape
    inner = 2 if n % 2 == 0 else 1
    outer = n // inner
    half = jnp.bfloat16
    full = lambda *shape: pltpu.VMEM(shape, half)
    dma = lambda *shape: pltpu.SemaphoreType.DMA(shape)
    anywhere = pl.BlockSpec(memory_space=pl.ANY)
    return pl.pallas_call(
        functools.partial(fused_body, n, inner),
        out_shape=[
            jax.ShapeDtypeStruct((rows, chans), half),
            jax.ShapeDtypeStruct((n, toks, chans), half),
            jax.ShapeDtypeStruct((n, toks, chans), half),
            jax.ShapeDtypeStruct((2 * toks, chans), half),
        ],
        in_specs=[pl.BlockSpec(memory_space=pltpu.SMEM)] * 2
        + [pl.BlockSpec(memory_space=pltpu.VMEM)] * 3
        + [anywhere] * 7,
        out_specs=[anywhere] * 4,
        scratch_shapes=[
            full(rows, chans), full(rows, chans), full(rows, chans),
            pltpu.VMEM((chans, taps), jnp.float32),
            full(taps, chans), full(taps, chans), full(rows, chans), full(rows, chans),
            full(n, toks, chans), full(n, toks, chans), full(n, 2 * toks, chans),
            full(n, toks, chans), full(n, toks, chans), full(n, 2 * toks, chans),
            full(outer, 2 * toks, chans), full(outer, 2 * toks, chans),
            full(outer, 2 * toks, chans), full(outer, 2 * toks, chans), full(2 * toks, chans),
            dma(5), dma(6), dma(2), dma(2, n), dma(2, n), dma(2, n), dma(2, n),
            dma(outer + 1), dma(outer + 1), dma(outer + 1), dma(outer + 1),
            dma(outer), dma(outer), dma(outer), dma(outer),
            dma(outer), dma(outer), dma(outer), dma(outer),
        ],
        compiler_params=pltpu.CompilerParams(
            collective_id=0, has_side_effects=True, vmem_limit_bytes=48 * 2**20
        ),
        name="fused",
    )(info, temps, *transforms(taps), gate, keys, values, filters, *sent)


def combine_body(blocks_ref, within_ref, a_ref, b_ref, x_ref, o_ref):
    at = within_ref[pl.program_id(0)]
    toks = o_ref.shape[1]

    @pl.when(at == 0)
    def _():
        o_ref[...] = a_ref[...]

    @pl.when(at == 1)
    def _():
        o_ref[...] = b_ref[...]

    @pl.when(at == 2)
    def _():
        o_ref[0] = x_ref[:toks]

    @pl.when(at == 3)
    def _():
        o_ref[0] = x_ref[toks:]


def combine(blocks, within, parts, windows):
    _, toks, chans = parts[0].shape
    moving = pl.BlockSpec((1, toks, chans), lambda w, b, s: (b[w], 0, 0))
    still = pl.BlockSpec((2 * toks, chans), lambda w, b, s: (0, 0))
    return pl.pallas_call(
        combine_body,
        grid_spec=pltpu.PrefetchScalarGridSpec(
            num_scalar_prefetch=2,
            grid=(windows,),
            in_specs=[moving, moving, still],
            out_specs=pl.BlockSpec((1, toks, chans), lambda w, b, s: (w, 0, 0)),
        ),
        out_shape=jax.ShapeDtypeStruct((windows, toks, chans), jnp.bfloat16),
        name="combine",
    )(blocks, within, *parts)


def shards(gate_stream, key_stream, value_stream, filters, temps, queries, blocks, sites):
    rows, chans = gate_stream.shape
    count = lax.axis_size("pos")
    me = lax.axis_index("pos")
    windows = blocks.shape[0]

    order = jnp.arange(windows, dtype=jnp.int32)
    same = (blocks[:, None] == blocks[None, :]) & (order[None, :] < order[:, None])
    within = jnp.sum(same, axis=1, dtype=jnp.int32)
    target = jnp.concatenate(
        [jnp.arange(2 * count, dtype=jnp.int32), jnp.full((2,), 2 * count, jnp.int32)
         + jnp.arange(2, dtype=jnp.int32)]
    )
    place = jnp.where(within < 2, within * count + blocks, 2 * count + within - 2)
    hit = place[None, :] == target[:, None]
    idx = jnp.sum(jnp.where(hit, order[None, :], 0), axis=1, dtype=jnp.int32)
    slots = jnp.arange(4, dtype=jnp.int32)
    mine = (blocks == me)[None, :] & (within[None, :] == slots[:, None])
    found = jnp.sum(mine, axis=1, dtype=jnp.int32)
    offsets = jnp.sum(jnp.where(mine, sites[None, :] - me * rows, 0), axis=1, dtype=jnp.int32)
    offsets = jnp.where(found > 0, offsets, rows)
    info = jnp.concatenate([offsets, found[2:3]])

    sent = dispatch(idx, queries, count)
    hyena_out, back0, back1, backx = fused(
        info, temps, (gate_stream, key_stream, value_stream), filters, sent
    )
    attended = combine(blocks, within, (back0, back1, backx), windows)
    return (hyena_out, attended)


def solution(mesh):
    placed = (
        P(("groups", "pos"), "mp"),
        P(("groups", "pos"), "mp"),
        P(("groups", "pos"), "mp"),
        P("mp", None),
        P("mp"),
        P("groups", "pos", "mp"),
        P("groups"),
        P("groups"),
    )
    return jax.shard_map(
        shards,
        mesh=mesh,
        in_specs=placed,
        out_specs=(P(("groups", "pos"), "mp"), P("groups", "pos", "mp")),
        check_vma=False,
    )
```

time: 282 us -> 184 us (0.65); the launches traced: 278 us -> 184 us
  waiting for transfers between devices: 140 us -> 0 us
  Pallas kernels: 59.8 us -> 170 us
  blocking collectives: 34.3 us -> 0 us
  starting transfers between devices: 25.4 us -> 0 us
  between operations: 13.8 us -> 0.73 us
  local copies, waits for them, and re-layouts: 1.51 us -> 7.99 us
    pallas_call x6 -> x1, Pallas kernels: 41.5 us -> 152 us  [fused(): pl.pallas_call(functools.partial(fused_body, n, inner), out_shape=[jax.Sh...]
    reduce_scatter x2 -> x0, waiting for transfers between devices: 65 us -> none  [the longest x1 65 us: shards(): lax.psum_scatter(attend(3, info, temps, got3, hyena_out), 'pos', scatter_...]
    all_to_all x3 -> x0, waiting for transfers between devices: 49.3 us -> none  [the longest x1 31.8 us: shards(): got1 = lax.all_to_all(sent[1], 'pos', 0, 0, tiled=True)]
    all_to_all x1 -> x0, blocking collectives: 34.3 us -> none  [shards(): lax.all_to_all(attend(0, info, temps, got0, hyena_out), 'pos', 0, 0, tile...]
    ppermute x1 -> x0, waiting for transfers between devices: 24.9 us -> none  [shards(): earlier = lax.ppermute(tail, 'pos', [(i, i + 1) for i in range(count - 1)])]
    all_to_all x3 -> x0, starting transfers between devices: 21.9 us -> none  [the longest x1 11.5 us: shards(): lax.all_to_all(attend(1, info, temps, got1, hyena_out), 'pos', 0, 0, tile...]
    unnamed x14 -> x27, local copies, waits for them, and re-layouts: 0.86 us -> 7.4 us
    ppermute x1 -> x0, starting transfers between devices: 3.37 us -> none  [shards(): earlier = lax.ppermute(tail, 'pos', [(i, i + 1) for i in range(count - 1)])]
  transfers between devices with their start and end apart: 8 -> 0, of which waited for: 4 -> 0; matrix products, arithmetic and copies ran while one was open for 1% -> 0% of each run, Pallas kernels for 15% -> 0%
where the time goes in v2:
time: 184 us
  Pallas kernels  170 us (92%)
  local copies, waits for them, and re-layouts  7.99 us (4%)
  other arithmetic  4.44 us (2%)
    pallas_call x1, Pallas kernels, fused(): pl.pallas_call(functools.partial(fused_body, n, inner), out_shape=[jax.Sh...  152 us
    pallas_call x1, Pallas kernels, combine(): pl.pallas_call(combine_body, grid_spec=pltpu.PrefetchScalarGridSpec(num_s...  10.8 us
    pallas_call x1, Pallas kernels, dispatch(): pl.pallas_call(dispatch_body, grid_spec=pltpu.PrefetchScalarGridSpec(num_...  7.73 us
    unnamed x27, local copies, waits for them, and re-layouts  7.4 us

profile of v2, /device:TPU:6, one launch (start us, length us, event | category | flops | bytes accessed | tf_op | source)
XLA Modules:
  0.0 183.6 jit_solution(6132441593386035575)
XLA Ops:
  0.6 0.7 broadcast_compare_fusion
  1.3 0.7 broadcast_subtract_fusion
  2.0 0.9 convert_reduce_fusion.within_ref
  2.9 0.0 copy-start.12
  2.9 0.1 select_reduce_fusion.1
  3.0 0.6 slice.3
  3.6 0.7 pad_add_fusion.info_ref
  4.3 0.7 compare_select_fusion
  5.0 0.1 pad_add_fusion.1
  5.1 0.6 select_reduce_fusion.idx_ref
  5.7 0.0 copy-start.2
  5.7 0.0 copy-start.7
  5.7 0.0 copy-start.8
  5.7 0.0 copy-start.9
  5.7 0.0 copy-start.10
  5.7 7.7 %dispatch.1 = (bf16[8,32,2048]{2,1,0:T(8,128)(2,1)}, bf16[8,32,2048]{2,1,0:T(8,128)(2,1)}, bf16[64,2048]{1,0:T(8,128)(2,1)}) custom-call(s32[18]{0:T(128)} %select_reduce_fusion.idx_ref, bf16[16,32,2048]{2,1,0:T(8,128)(2,1)} %d_ref.1, bf16[16,32,2048]{2,1,0:T(8,128)(2,1)} %d_ref.1, bf16[16,32,2048]{2,1,0:T(8,128)(2,1)} %d_ref.1, bf16[16,32,2048]{2,1,0:T(8,128)(2,1)} %d_ref.1), custom_call_target="tpu_custom_call" | custom-call | tf_op jit(solution)/shard_map/dispatch/pallas_call | solution.py:56
  13.4 0.0 copy-done.12
  13.4 0.0 copy-done.2
  13.4 0.0 copy-done.7
  13.5 0.0 copy-done.8
  13.5 0.0 copy-done.9
  13.5 0.0 copy-done.10
  13.5 0.0 copy-start.3
  13.5 1.2 copy-done.3
  14.7 0.0 copy-start.4
  14.7 1.2 copy-done.4
  15.9 0.0 copy-start.6
  15.9 0.9 copy-done.6
  16.9 151.8 %fused.1 = (bf16[512,2048]{1,0:T(8,128)(2,1)}, bf16[8,32,2048]{2,1,0:T(8,128)(2,1)S(1)}, bf16[8,32,2048]{2,1,0:T(8,128)(2,1)S(1)}, bf16[64,2048]{1,0:T(8,128)(2,1)S(1)}) custom-call(s32[5]{0:T(128)S(1)} %pad_add_fusion.info_ref, f32[16]{0:T(128)S(1)} %copy-done.10, bf16[256,256]{1,0:T(8,128)(2,1)S(1)} %copy-done.8, bf16[256,256]{1,0:T(8,128)(2,1)S(1)} %copy-done.7, ...), custom_call_target="tpu_custom_call" | custom-call | tf_op jit(solution)/shard_map/fused/pallas_call | solution.py:404
  168.7 0.0 copy-start
  168.7 1.0 copy-done
  169.7 0.0 copy-start.1
  169.7 1.0 copy-done.1
  170.7 0.0 copy-start.5
  170.7 0.7 copy-done.5
  171.4 0.0 copy-start.11
  171.4 10.8 %combine.1 = bf16[16,32,2048]{2,1,0:T(8,128)(2,1)} custom-call(s32[16]{0:T(128)} %blocks_ref.1, s32[16]{0:T(128)} %copy-done.12, bf16[8,32,2048]{2,1,0:T(8,128)(2,1)} %copy-done, bf16[8,32,2048]{2,1,0:T(8,128)(2,1)} %copy-done.1, bf16[64,2048]{1,0:T(8,128)(2,1)} %copy-done.5), custom_call_target="tpu_custom_call" | custom-call | tf_op jit(solution)/shard_map/combine/pallas_call | solution.py:461
  182.2 0.0 copy-done.11
  182.2 1.3 copy.14
  (3 shorter events, 0.0 us)
Async XLA Ops:
  2.9 10.6 %copy-start.12 = (s32[16]{0:T(128)}, s32[16]{0:T(128)S(1)}, u32[]{:S(2)}) copy-start(s32[16]{0:T(128)S(1)} %convert_reduce_fusion.within_ref) | copy-start | bytes 196
  5.7 7.8 %copy-start.2 = (f32[2048,128]{1,0:T(8,128)S(1)}, f32[2048,128]{1,0:T(8,128)}, u32[]{:S(2)}) copy-start(f32[2048,128]{1,0:T(8,128)} %f_hbm.1) | copy-start | bytes 3145732
  5.7 7.8 %copy-start.7 = (bf16[256,256]{1,0:T(8,128)(2,1)S(1)}, bf16[256,256]{1,0:T(8,128)(2,1)}, u32[]{:S(2)}) copy-start(bf16[256,256]{1,0:T(8,128)(2,1)} %constant.28.clone.short_ref) | copy-start | bytes 393220
  5.7 7.8 %copy-start.8 = (bf16[256,256]{1,0:T(8,128)(2,1)S(1)}, bf16[256,256]{1,0:T(8,128)(2,1)}, u32[]{:S(2)}) copy-start(bf16[256,256]{1,0:T(8,128)(2,1)} %constant.27.clone.fwd_ref) | copy-start | bytes 393220
  5.7 7.8 %copy-start.9 = (bf16[128,256]{1,0:T(8,128)(2,1)S(1)}, bf16[128,256]{1,0:T(8,128)(2,1)}, u32[]{:S(2)}) copy-start(bf16[128,256]{1,0:T(8,128)(2,1)} %constant.29.clone.inv_ref) | copy-start | bytes 196612
  5.7 7.8 %copy-start.10 = (f32[16]{0:T(128)S(1)}, f32[16]{0:T(128)}, u32[]{:S(2)}) copy-start(f32[16]{0:T(128)} %temps_ref.1) | copy-start | bytes 196
  13.5 1.2 copy-start.3
  14.7 1.2 copy-start.4
  15.9 0.9 copy-start.6
  168.7 1.0 copy-start
  169.7 1.0 copy-start.1
  170.7 0.7 copy-start.5
  171.4 10.8 %copy-start.11 = (bf16[512,2048]{1,0:T(8,128)(2,1)S(1)}, bf16[512,2048]{1,0:T(8,128)(2,1)}, u32[]{:S(2)}) copy-start(bf16[512,2048]{1,0:T(8,128)(2,1)} %get-tuple-element.20) | copy-start | bytes 6291460

commit v3 on v2

--- a/solution.py
+++ b/solution.py
@@ -29,50 +29,57 @@
     return block * lax.rsqrt(jnp.mean(block * block, axis=-1, keepdims=True) + 1e-06)
 
 
-def dispatch_body(idx_ref, a_ref, b_ref, c_ref, d_ref, oa_ref, ob_ref, ox_ref):
-    toks = a_ref.shape[1]
-
-    def norm(src, dst, first):
-        for h in range(dst.shape[-1] // HEAD_DIM):
-            at = slice(h * HEAD_DIM, (h + 1) * HEAD_DIM)
-            dst[first, at] = unit(src[0, :, at].astype(jnp.float32)).astype(jnp.bfloat16)
-
-    norm(a_ref, oa_ref.at[0], slice(0, toks))
-    norm(b_ref, ob_ref.at[0], slice(0, toks))
-
-    @pl.when(pl.program_id(0) == 0)
-    def _():
-        norm(c_ref, ox_ref, slice(0, toks))
-        norm(d_ref, ox_ref, slice(toks, 2 * toks))
-
-
-def dispatch(idx, queries, count):
-    windows, toks, chans = queries.shape
-    source = lambda at: pl.BlockSpec((1, toks, chans), lambda g, i: (i[at(g)], 0, 0))
-    moving = pl.BlockSpec((1, toks, chans), lambda g, i: (g, 0, 0))
-    still = pl.BlockSpec((2 * toks, chans), lambda g, i: (0, 0))
-    big = jax.ShapeDtypeStruct((count, toks, chans), jnp.bfloat16)
-    small = jax.ShapeDtypeStruct((2 * toks, chans), jnp.bfloat16)
+def route_body(n, rows, blocks_ref, sites_ref, o_ref, seen):
+    windows = blocks_ref.shape[0]
+    me = lax.axis_index("pos")
+    info = 2 * n + 2 + windows
+
+    def clear(i, carry):
+        o_ref[i] = 0
+        return carry
+
+    def fresh(i, carry):
+        seen[i] = 0
+        return carry
+
+    def one(w, carry):
+        block = blocks_ref[w]
+        within = seen[block]
+        seen[block] = within + 1
+        place = jnp.where(within < 2, within * n + block, 2 * n + within - 2)
+        o_ref[place] = w
+        o_ref[2 * n + 2 + w] = place
+        mine = block == me
+        o_ref[info + within] = jnp.where(mine, sites_ref[w] - me * rows, o_ref[info + within])
+        o_ref[info + 4] = jnp.where(mine & (within == 2), 1, o_ref[info + 4])
+        return carry
+
+    lax.fori_loop(0, 2 * n + 2, clear, 0)
+    lax.fori_loop(0, n, fresh, 0)
+    for slot in range(4):
+        o_ref[info + slot] = rows
+    o_ref[info + 4] = 0
+    lax.fori_loop(0, windows, one, 0)
+
+
+def route(blocks, sites, n, rows):
+    windows = blocks.shape[0]
+    smem = pl.BlockSpec(memory_space=pltpu.SMEM)
     return pl.pallas_call(
-        dispatch_body,
-        grid_spec=pltpu.PrefetchScalarGridSpec(
-            num_scalar_prefetch=1,
-            grid=(count,),
-            in_specs=[
-                source(lambda g: g), source(lambda g: count + g),
-                source(lambda g: 2 * count), source(lambda g: 2 * count + 1),
-            ],
-            out_specs=[moving, moving, still],
-        ),
-        out_shape=[big, big, small],
-        name="dispatch",
-    )(idx, queries, queries, queries, queries)
+        functools.partial(route_body, n, rows),
+        out_shape=jax.ShapeDtypeStruct((2 * n + windows + 7,), jnp.int32),
+        in_specs=[smem, smem],
+        out_specs=smem,
+        scratch_shapes=[pltpu.SMEM((n,), jnp.int32)],
+        name="route",
+    )(blocks, sites)
 
 
 def fused_body(
-    n, inner, info_ref, temps_ref, fwd_ref, short_ref, inv_ref, g_hbm, k_hbm, v_hbm, f_hbm,
-    d0_hbm, d1_hbm, e_hbm, hyena_out, back0, back1, backx,
-    gv, kv, vv, fv, tail, halo, hy, keyed, q0, q1, qx, o0, o1, ox, acc, side, rise, fall, last,
+    n, inner, plan_ref, temps_ref, fwd_ref, short_ref, inv_ref, g_hbm, k_hbm, v_hbm, f_hbm,
+    x_hbm, hyena_out, out_ref,
+    gv, kv, vv, fv, qv, s0, s1, tail, halo, hy, keyed, q0, q1, qx, o0, o1, ox, acc, side, rise,
+    fall, back,
     load, local, halo_sem, go_send, go_recv, ret_send, ret_recv, up_send, up_recv,
     down_send, down_recv, part_send, part_recv, rpart_send, rpart_recv,
     rup_send, rup_recv, rdown_send, rdown_recv,
@@ -84,6 +91,8 @@
     taps = fv.shape[1]
     toks = q0.shape[1]
     wide = 2 * HEAD_DIM
+    windows = qv.shape[0]
+    info = 2 * n + 2 + windows
 
     def remote(src, dst, send, recv, who):
         return pltpu.make_async_remote_copy(
@@ -94,17 +103,19 @@
     loads = [
         pltpu.make_async_copy(src, dst, load.at[i])
         for i, (src, dst) in enumerate(
-            ((k_hbm, kv), (v_hbm, vv), (e_hbm, qx.at[me]), (g_hbm, gv), (f_hbm, fv))
+            ((k_hbm, kv), (v_hbm, vv), (x_hbm, qv), (g_hbm, gv), (f_hbm, fv))
         )
     ]
     for copy in loads:
         copy.start()
-    own = [
-        pltpu.make_async_copy(d0_hbm.at[me], q0.at[me], local.at[0]),
-        pltpu.make_async_copy(d1_hbm.at[me], q1.at[me], local.at[1]),
-    ]
-    for copy in own:
-        copy.start()
+
+    def norm(slot, dst, at, first):
+        w = plan_ref[slot]
+        for h in range(chans // HEAD_DIM):
+            cols = slice(h * HEAD_DIM, (h + 1) * HEAD_DIM)
+            dst[at, first:first + toks, cols] = unit(
+                qv[w, :, cols].astype(jnp.float32)
+            ).astype(jnp.bfloat16)
 
     barrier = pltpu.get_barrier_semaphore()
     for off in range(1, n):
@@ -124,6 +135,8 @@
         halo_copy.start()
 
     loads[2].wait()
+    norm(2 * n, qx, me, 0)
+    norm(2 * n + 1, qx, me, toks)
 
     def across(z):
         slot = z * inner + yi
@@ -173,13 +186,23 @@
         to = (me + off) % n
         return remote(src.at[to], dst.at[me], go_send.at[slot, off], go_recv.at[slot, off], to)
 
-    def back_copy(slot, src, dst, off):
+    def back_copy(slot, src, off):
         to = (me + off) % n
-        return remote(src.at[to], dst.at[me], ret_send.at[slot, off], ret_recv.at[slot, off], to)
+        return remote(src.at[to], back.at[slot * n + me], ret_send.at[slot, off], ret_recv.at[slot, off], to)
 
     gather_send(1)
-    for off in range(1, n):
-        out_copy(0, d0_hbm, q0, off).start()
+
+    def send(slot, buf, dst):
+        def one(off, carry):
+            to = (me + off) % n
+            norm(slot * n + to, buf, to, 0)
+            out_copy(slot, buf, dst, off).start()
+            return carry
+
+        lax.fori_loop(1, n, one, 0)
+        norm(slot * n + me, dst, me, 0)
+
+    send(0, s0, q0)
 
     loads[3].wait()
     loads[4].wait()
@@ -228,14 +251,13 @@
     hyena_copy = pltpu.make_async_copy(hy, hyena_out, local.at[2])
     hyena_copy.start()
 
-    for off in range(1, n):
-        out_copy(1, d1_hbm, q1, off).start()
-    for step in range(1, outer):
-        gather_recv(step)
-        gather_send(step + 1)
+    if outer > 1:
+        gather_recv(1)
+        gather_send(2)
+    send(1, s1, q1)
 
     def attend(slot, q, o, first, hot):
-        off = info_ref[slot]
+        off = plan_ref[info + slot]
         seen = off * hot
 
         def one(c, carry):
@@ -263,19 +285,30 @@
 
         lax.fori_loop(0, tiles, one, 0)
 
-    own[0].wait()
     for off in range(1, n):
-        out_copy(0, d0_hbm, q0, off).wait_recv()
+        out_copy(0, s0, q0, off).wait_recv()
     attend(0, q0, o0, 0, 1)
+    if outer > 2:
+        gather_recv(2)
+        gather_send(3)
     for off in range(1, n):
-        back_copy(0, o0, back0, off).start()
-    mine0 = pltpu.make_async_copy(o0.at[me], back0.at[me], local.at[3])
+        back_copy(0, o0, off).start()
+    mine0 = pltpu.make_async_copy(o0.at[me], back.at[me], local.at[0])
     mine0.start()
 
+    for off in range(1, n):
+        out_copy(1, s1, q1, off).wait_recv()
+    attend(1, q1, o1, 0, 1)
+    mine1 = pltpu.make_async_copy(o1.at[me], back.at[n + me], local.at[1])
+    mine1.start()
+
+    for step in range(3, outer):
+        gather_recv(step)
+        gather_send(step + 1)
     if inner == 2:
         for z in range(outer):
             across(z).wait_recv()
-    hot = info_ref[4]
+    hot = plan_ref[info + 4]
     attend(2, qx, ox, 0, hot)
     attend(3, qx, ox, toks, hot)
 
@@ -288,15 +321,6 @@
     if inner == 2:
         for z in range(outer):
             swap(z).start()
-
-    own[1].wait()
-    for off in range(1, n):
-        out_copy(1, d1_hbm, q1, off).wait_recv()
-    attend(1, q1, o1, 0, 1)
-    for off in range(1, n):
-        back_copy(1, o1, back1, off).start()
-    mine1 = pltpu.make_async_copy(o1.at[me], back1.at[me], local.at[4])
-    mine1.start()
 
     def lift(z):
         to = jnp.minimum(zi + 1, outer - 1) * inner + yi
@@ -333,32 +357,48 @@
 
             drop(z).start()
 
-    for step in range(outer - 1):
-        reduce_up(outer - 1 - step)
-        reduce_down(step)
-    last[...] = acc[zi]
+    hops = max(outer - 1, 1)
+    cuts = [1 + (n - 1) * i // hops for i in range(hops + 1)]
+    for step in range(hops):
+        if outer > 1:
+            reduce_up(outer - 1 - step)
+            reduce_down(step)
+        for off in range(cuts[step], cuts[step + 1]):
+            back_copy(1, o1, off).start()
+    back[2 * n] = acc[zi, :toks]
+    back[2 * n + 1] = acc[zi, toks:]
+
+    def add(ref):
+        back[2 * n] = back[2 * n] + ref[zi, :toks]
+        back[2 * n + 1] = back[2 * n + 1] + ref[zi, toks:]
 
     @pl.when(zi > 0)
     def _():
         lift(zi).wait_recv()
-        last[...] = last[...] + rise[zi]
+        add(rise)
 
     @pl.when(zi < outer - 1)
     def _():
         drop(zi).wait_recv()
-        last[...] = last[...] + fall[zi]
-
-    end = pltpu.make_async_copy(last, backx, local.at[5])
-    end.start()
-
+        add(fall)
+
+    mine0.wait()
+    mine1.wait()
     for off in range(1, n):
-        back_copy(0, o0, back0, off).wait_recv()
-        back_copy(1, o1, back1, off).wait_recv()
+        back_copy(0, o0, off).wait_recv()
+        back_copy(1, o1, off).wait_recv()
+
+    def pick(w, carry):
+        out_ref[w] = back[plan_ref[2 * n + 2 + w]]
+        return carry
+
+    lax.fori_loop(0, windows, pick, 0)
+
     for off in range(1, n):
-        out_copy(0, d0_hbm, q0, off).wait_send()
-        out_copy(1, d1_hbm, q1, off).wait_send()
-        back_copy(0, o0, back0, off).wait_send()
-        back_copy(1, o1, back1, off).wait_send()
+        out_copy(0, s0, q0, off).wait_send()
+        out_copy(1, s1, q1, off).wait_send()
+        back_copy(0, o0, off).wait_send()
+        back_copy(1, o1, off).wait_send()
 
     @pl.when(me < n - 1)
     def _():
@@ -386,15 +426,14 @@
         def _(z=z):
             drop(z).wait_send()
 
-    for copy in (hyena_copy, mine0, mine1, end):
-        copy.wait()
-
-
-def fused(info, temps, streams, filters, sent):
+    hyena_copy.wait()
+
+
+def fused(plan, temps, streams, filters, queries, n):
     gate, keys, values = streams
     rows, chans = gate.shape
     taps = filters.shape[1]
-    n, toks, _ = sent[0].shape
+    windows, toks, _ = queries.shape
     inner = 2 if n % 2 == 0 else 1
     outer = n // inner
     half = jnp.bfloat16
@@ -405,101 +444,40 @@
         functools.partial(fused_body, n, inner),
         out_shape=[
             jax.ShapeDtypeStruct((rows, chans), half),
-            jax.ShapeDtypeStruct((n, toks, chans), half),
-            jax.ShapeDtypeStruct((n, toks, chans), half),
-            jax.ShapeDtypeStruct((2 * toks, chans), half),
+            jax.ShapeDtypeStruct((windows, toks, chans), half),
         ],
         in_specs=[pl.BlockSpec(memory_space=pltpu.SMEM)] * 2
         + [pl.BlockSpec(memory_space=pltpu.VMEM)] * 3
-        + [anywhere] * 7,
-        out_specs=[anywhere] * 4,
+        + [anywhere] * 5,
+        out_specs=[anywhere, pl.BlockSpec(memory_space=pltpu.VMEM)],
         scratch_shapes=[
             full(rows, chans), full(rows, chans), full(rows, chans),
             pltpu.VMEM((chans, taps), jnp.float32),
+            full(windows, toks, chans), full(n, toks, chans), full(n, toks, chans),
             full(taps, chans), full(taps, chans), full(rows, chans), full(rows, chans),
             full(n, toks, chans), full(n, toks, chans), full(n, 2 * toks, chans),
             full(n, toks, chans), full(n, toks, chans), full(n, 2 * toks, chans),
             full(outer, 2 * toks, chans), full(outer, 2 * toks, chans),
-            full(outer, 2 * toks, chans), full(outer, 2 * toks, chans), full(2 * toks, chans),
-            dma(5), dma(6), dma(2), dma(2, n), dma(2, n), dma(2, n), dma(2, n),
+            full(outer, 2 * toks, chans), full(outer, 2 * toks, chans),
+            full(2 * n + 2, toks, chans),
+            dma(5), dma(3), dma(2), dma(2, n), dma(2, n), dma(2, n), dma(2, n),
             dma(outer + 1), dma(outer + 1), dma(outer + 1), dma(outer + 1),
             dma(outer), dma(outer), dma(outer), dma(outer),
             dma(outer), dma(outer), dma(outer), dma(outer),
         ],
         compiler_params=pltpu.CompilerParams(
-            collective_id=0, has_side_effects=True, vmem_limit_bytes=48 * 2**20
+            collective_id=0, has_side_effects=True, vmem_limit_bytes=67043328
         ),
         name="fused",
-    )(info, temps, *transforms(taps), gate, keys, values, filters, *sent)
-
-
-def combine_body(blocks_ref, within_ref, a_ref, b_ref, x_ref, o_ref):
-    at = within_ref[pl.program_id(0)]
-    toks = o_ref.shape[1]
-
-    @pl.when(at == 0)
-    def _():
-        o_ref[...] = a_ref[...]
-
-    @pl.when(at == 1)
-    def _():
-        o_ref[...] = b_ref[...]
-
-    @pl.when(at == 2)
-    def _():
-        o_ref[0] = x_ref[:toks]
-
-    @pl.when(at == 3)
-    def _():
-        o_ref[0] = x_ref[toks:]
-
-
-def combine(blocks, within, parts, windows):
-    _, toks, chans = parts[0].shape
-    moving = pl.BlockSpec((1, toks, chans), lambda w, b, s: (b[w], 0, 0))
-    still = pl.BlockSpec((2 * toks, chans), lambda w, b, s: (0, 0))
-    return pl.pallas_call(
-        combine_body,
-        grid_spec=pltpu.PrefetchScalarGridSpec(
-            num_scalar_prefetch=2,
-            grid=(windows,),
-            in_specs=[moving, moving, still],
-            out_specs=pl.BlockSpec((1, toks, chans), lambda w, b, s: (w, 0, 0)),
-        ),
-        out_shape=jax.ShapeDtypeStruct((windows, toks, chans), jnp.bfloat16),
-        name="combine",
-    )(blocks, within, *parts)
+    )(plan, temps, *transforms(taps), gate, keys, values, filters, queries)
 
 
 def shards(gate_stream, key_stream, value_stream, filters, temps, queries, blocks, sites):
-    rows, chans = gate_stream.shape
     count = lax.axis_size("pos")
-    me = lax.axis_index("pos")
-    windows = blocks.shape[0]
-
-    order = jnp.arange(windows, dtype=jnp.int32)
-    same = (blocks[:, None] == blocks[None, :]) & (order[None, :] < order[:, None])
-    within = jnp.sum(same, axis=1, dtype=jnp.int32)
-    target = jnp.concatenate(
-        [jnp.arange(2 * count, dtype=jnp.int32), jnp.full((2,), 2 * count, jnp.int32)
-         + jnp.arange(2, dtype=jnp.int32)]
+    plan = route(blocks, sites, count, gate_stream.shape[0])
+    return tuple(
+        fused(plan, temps, (gate_stream, key_stream, value_stream), filters, queries, count)
     )
-    place = jnp.where(within < 2, within * count + blocks, 2 * count + within - 2)
-    hit = place[None, :] == target[:, None]
-    idx = jnp.sum(jnp.where(hit, order[None, :], 0), axis=1, dtype=jnp.int32)
-    slots = jnp.arange(4, dtype=jnp.int32)
-    mine = (blocks == me)[None, :] & (within[None, :] == slots[:, None])
-    found = jnp.sum(mine, axis=1, dtype=jnp.int32)
-    offsets = jnp.sum(jnp.where(mine, sites[None, :] - me * rows, 0), axis=1, dtype=jnp.int32)
-    offsets = jnp.where(found > 0, offsets, rows)
-    info = jnp.concatenate([offsets, found[2:3]])
-
-    sent = dispatch(idx, queries, count)
-    hyena_out, back0, back1, backx = fused(
-        info, temps, (gate_stream, key_stream, value_stream), filters, sent
-    )
-    attended = combine(blocks, within, (back0, back1, backx), windows)
-    return (hyena_out, attended)
 
 
 def solution(mesh):

time: 184 us -> 181 us (0.984)
  other arithmetic: 4.44 us -> 0 us
  Pallas kernels: 170 us -> 174 us
  local copies, waits for them, and re-layouts: 7.99 us -> 4.63 us
    pallas_call x1, Pallas kernels: 152 us -> 172 us  [fused(): pl.pallas_call(functools.partial(fused_body, n, inner), out_shape=[jax.Sh...]
    pallas_call x2 -> x1, Pallas kernels: 18.6 us -> 1.65 us  [route(): pl.pallas_call(functools.partial(route_body, n, rows), out_shape=jax.Shap...]
    unnamed x27 -> x4, local copies, waits for them, and re-layouts: 7.4 us -> 4.63 us
where the time goes in v3:
time: 181 us; the launch traced here: 179 us
  Pallas kernels  174 us (96%)
  local copies, waits for them, and re-layouts  4.63 us (3%)
    pallas_call x1, Pallas kernels, fused(): pl.pallas_call(functools.partial(fused_body, n, inner), out_shape=[jax.Sh...  172 us
    unnamed x4, local copies, waits for them, and re-layouts  4.63 us

profile of v3, /device:TPU:6, one launch (start us, length us, event | category | flops | bytes accessed | tf_op | source)
XLA Modules:
  0.0 178.9 jit_solution(12594929036514817506)
XLA Ops:
  0.6 1.7 route.1.plan_ref
  2.3 172.0 %fused.1 = (bf16[512,2048]{1,0:T(8,128)(2,1)}, bf16[16,32,2048]{2,1,0:T(8,128)(2,1)}) custom-call(s32[39]{0:T(128)} %route.1.plan_ref, f32[16]{0:T(128)} %temps_ref.1, bf16[256,256]{1,0:T(8,128)(2,1)} %constant.6.clone.fwd_ref, bf16[256,256]{1,0:T(8,128)(2,1)} %constant.7.clone.short_ref, bf16[128,256]{1,0:T(8,128)(2,1)} %constant.8.clone.inv_ref, ...), custom_call_target="tpu_custom_call" | custom-call | tf_op jit(solution)/shard_map/fused/pallas_call | solution.py:443
  174.3 0.0 copy-start
  174.3 3.3 %copy.15 = bf16[512,2048]{1,0:T(8,128)(2,1)} copy(bf16[512,2048]{1,0:T(8,128)(2,1)} %get-tuple-element.4) | data formatting | bytes 4194304
  177.6 0.0 copy-done
  177.6 1.3 copy.16
Async XLA Ops:
  174.3 3.3 %copy-start = (bf16[16,32,2048]{2,1,0:T(8,128)(2,1)S(1)}, bf16[16,32,2048]{2,1,0:T(8,128)(2,1)}, u32[]{:S(2)}) copy-start(bf16[16,32,2048]{2,1,0:T(8,128)(2,1)} %get-tuple-element.5) | copy-start | bytes 6291460

commit v4 on v3

--- a/solution.py
+++ b/solution.py
@@ -130,10 +130,6 @@
     tail[...] = (kv[at].astype(jnp.float32) * vv[at].astype(jnp.float32)).astype(jnp.bfloat16)
     halo_copy = remote(tail, halo, halo_sem.at[0], halo_sem.at[1], (me + 1) % n)
 
-    @pl.when(me < n - 1)
-    def _():
-        halo_copy.start()
-
     loads[2].wait()
     norm(2 * n, qx, me, 0)
     norm(2 * n + 1, qx, me, toks)
@@ -192,17 +188,30 @@
 
     gather_send(1)
 
-    def send(slot, buf, dst):
+    def send(slot, buf, dst, low, high):
         def one(off, carry):
             to = (me + off) % n
             norm(slot * n + to, buf, to, 0)
             out_copy(slot, buf, dst, off).start()
             return carry
 
-        lax.fori_loop(1, n, one, 0)
-        norm(slot * n + me, dst, me, 0)
-
-    send(0, s0, q0)
+        lax.fori_loop(low, high, one, 0)
+
+    hops = max(outer - 1, 1)
+    cuts = [1 + (n - 1) * i // hops for i in range(hops + 1)]
+    for step in range(hops):
+        send(0, s0, q0, cuts[step], cuts[step + 1])
+        if step == 0:
+            @pl.when(me < n - 1)
+            def _():
+                halo_copy.start()
+
+        if outer > 1:
+            gather_recv(step + 1)
+            gather_send(step + 2)
+    send(1, s1, q1, 1, n)
+    norm(me, q0, me, 0)
+    norm(n + me, q1, me, 0)
 
     loads[3].wait()
     loads[4].wait()
@@ -251,10 +260,6 @@
     hyena_copy = pltpu.make_async_copy(hy, hyena_out, local.at[2])
     hyena_copy.start()
 
-    if outer > 1:
-        gather_recv(1)
-        gather_send(2)
-    send(1, s1, q1)
 
     def attend(slot, q, o, first, hot):
         off = plan_ref[info + slot]
@@ -285,26 +290,6 @@
 
         lax.fori_loop(0, tiles, one, 0)
 
-    for off in range(1, n):
-        out_copy(0, s0, q0, off).wait_recv()
-    attend(0, q0, o0, 0, 1)
-    if outer > 2:
-        gather_recv(2)
-        gather_send(3)
-    for off in range(1, n):
-        back_copy(0, o0, off).start()
-    mine0 = pltpu.make_async_copy(o0.at[me], back.at[me], local.at[0])
-    mine0.start()
-
-    for off in range(1, n):
-        out_copy(1, s1, q1, off).wait_recv()
-    attend(1, q1, o1, 0, 1)
-    mine1 = pltpu.make_async_copy(o1.at[me], back.at[n + me], local.at[1])
-    mine1.start()
-
-    for step in range(3, outer):
-        gather_recv(step)
-        gather_send(step + 1)
     if inner == 2:
         for z in range(outer):
             across(z).wait_recv()
@@ -321,6 +306,12 @@
     if inner == 2:
         for z in range(outer):
             swap(z).start()
+
+    for off in range(1, n):
+        out_copy(0, s0, q0, off).wait_recv()
+    attend(0, q0, o0, 0, 1)
+    mine0 = pltpu.make_async_copy(o0.at[me], back.at[me], local.at[0])
+    mine0.start()
 
     def lift(z):
         to = jnp.minimum(zi + 1, outer - 1) * inner + yi
@@ -357,12 +348,24 @@
 
             drop(z).start()
 
-    hops = max(outer - 1, 1)
-    cuts = [1 + (n - 1) * i // hops for i in range(hops + 1)]
-    for step in range(hops):
+    def reduce(step):
         if outer > 1:
             reduce_up(outer - 1 - step)
             reduce_down(step)
+
+    reduce(0)
+    for off in range(1, n):
+        back_copy(0, o0, off).start()
+    for off in range(1, n):
+        out_copy(1, s1, q1, off).wait_recv()
+    attend(1, q1, o1, 0, 1)
+    mine1 = pltpu.make_async_copy(o1.at[me], back.at[n + me], local.at[1])
+    mine1.start()
+    rest = max(hops - 1, 1)
+    cuts = [1 + (n - 1) * i // rest for i in range(rest + 1)]
+    for step in range(rest):
+        if step + 1 < hops:
+            reduce(step + 1)
         for off in range(cuts[step], cuts[step + 1]):
             back_copy(1, o1, off).start()
     back[2 * n] = acc[zi, :toks]

time: 181 us -> 172 us (0.950)
  Pallas kernels: 174 us -> 163 us
    pallas_call x1, Pallas kernels: 172 us -> 162 us  [fused(): pl.pallas_call(functools.partial(fused_body, n, inner), out_shape=[jax.Sh...]
where the time goes in v4:
time: 172 us; the launch traced here: 169 us
  Pallas kernels  163 us (95%)
  local copies, waits for them, and re-layouts  4.63 us (3%)
    pallas_call x1, Pallas kernels, fused(): pl.pallas_call(functools.partial(fused_body, n, inner), out_shape=[jax.Sh...  162 us
    unnamed x4, local copies, waits for them, and re-layouts  4.63 us

profile of v4, /device:TPU:6, one launch (start us, length us, event | category | flops | bytes accessed | tf_op | source)
XLA Modules:
  0.0 168.6 jit_solution(16544986215614503114)
XLA Ops:
  0.6 1.6 route.1.plan_ref
  2.3 161.6 %fused.1 = (bf16[512,2048]{1,0:T(8,128)(2,1)}, bf16[16,32,2048]{2,1,0:T(8,128)(2,1)}) custom-call(s32[39]{0:T(128)} %route.1.plan_ref, f32[16]{0:T(128)} %temps_ref.1, bf16[256,256]{1,0:T(8,128)(2,1)} %constant.6.clone.fwd_ref, bf16[256,256]{1,0:T(8,128)(2,1)} %constant.7.clone.short_ref, bf16[128,256]{1,0:T(8,128)(2,1)} %constant.8.clone.inv_ref, ...), custom_call_target="tpu_custom_call" | custom-call | tf_op jit(solution)/shard_map/fused/pallas_call | solution.py:446
  163.9 0.0 copy-start
  163.9 3.3 %copy.15 = bf16[512,2048]{1,0:T(8,128)(2,1)} copy(bf16[512,2048]{1,0:T(8,128)(2,1)} %get-tuple-element.4) | data formatting | bytes 4194304
  167.2 0.0 copy-done
  167.2 1.3 copy.16
Async XLA Ops:
  163.9 3.3 %copy-start = (bf16[16,32,2048]{2,1,0:T(8,128)(2,1)S(1)}, bf16[16,32,2048]{2,1,0:T(8,128)(2,1)}, u32[]{:S(2)}) copy-start(bf16[16,32,2048]{2,1,0:T(8,128)(2,1)} %get-tuple-element.5) | copy-start | bytes 6291460
